TPU v7x, 256 devices: a whole 4x4x8 slice. The times are simulated.
256 devices in a mesh: gx: 64 (over z, x, core), gy: 4 (over y).
Axes of the slice: x: 4, y: 4, z: 8, core: 2. Of those that a mesh axis runs over, the one named last changes fastest.
Arguments:
- prior_warmth: float32 [16, 1024, 1024], P(None, 'gx', 'gy'), may hold values from -3 to 3
- prior_speed: float32 [16, 1024, 1024], P(None, 'gx', 'gy'), may hold values from -120 to 120
- energy_input: float32 [16, 1024, 1024], P(None, 'gx', 'gy'), may hold values from -120 to 120
Outputs:
- new_temperature: float32 [16, 1024, 1024], P(None, 'gx', 'gy')
- new_velocity: float32 [16, 1024, 1024], P(None, 'gx', 'gy')
All inputs are finite; a program needn't handle non-finite values.
Results may differ from a plain program's by a relative error of at most 0.0003.
Values sent between devices are 32-bit elements; how exact they have to be, the bound alone decides.
No kernel may reach another device: no remote copies, remote signals or barrier semaphores. Data moves between devices by JAX's collectives and lax.ppermute only.
A program may use at most 64 MiB of HBM per device.

v0:
```python
import functools

import jax
import jax.numpy as jnp
from jax import lax
from jax.experimental import pallas as pl
from jax.experimental.pallas import tpu as pltpu
from jax.sharding import PartitionSpec as P

diffusivity_slope = 0.3
stickiness_slope = 0.8
lifting_push = 8.0
span_strength = 1500.0
cross_strength = 1500.0
depth_strength = 2.0

SLOPES = (diffusivity_slope, -stickiness_slope)
PAIRS = 2
LANES = 128
CHUNKS = 8
SENT = 8
SIDES = 2
CROSS_SENT = 7


def block_sweep(steps, coefficient_at, source_at, strength, opens, keep):
    half = 0.5 * strength
    q_first = q_now = coefficient_at(0)
    numerator = source_at(0)
    delta = 1.0 + opens * (half * q_first)
    weight = jnp.ones_like(q_now)
    first_part = jnp.zeros_like(q_now)
    first_reach = jnp.zeros_like(q_now)
    for step in range(steps):
        if step == steps - 1:
            inverse = 1.0 / delta
            partial = numerator * inverse
            reach = weight * inverse
            keep(step, inverse, partial, reach)
            first_part = first_part + weight * partial
            first_reach = first_reach + weight * reach
            return (first_part, partial, first_reach, reach, inverse, q_first, q_now)
        q_next = coefficient_at(step + 1)
        face = half * (q_now + q_next)
        inverse = 1.0 / (delta + face)
        ratio = face * inverse
        partial = numerator * inverse
        reach = weight * inverse
        keep(step, ratio, partial, reach)
        first_part = first_part + weight * partial
        first_reach = first_reach + weight * reach
        delta = 1.0 + delta * ratio
        weight = weight * ratio
        numerator = source_at(step + 1) + face * partial
        q_now = q_next


def block_return(steps, kept_at, flux_low, flux_high, give):
    answer = None
    for step in reversed(range(steps)):
        ratio, partial, reach = kept_at(step)
        fixed = partial + reach * flux_low
        answer = fixed - ratio * flux_high if answer is None else fixed + ratio * answer
        give(step, answer)


def interface_flux(values, strength, rows):
    first_part, last_part, first_reach, cross_reach, last_reach, q_first, q_last = values
    row = lax.broadcasted_iota(jnp.int32, first_part.shape, 0)

    def following(value):
        return jnp.where(row < rows - 1, pltpu.roll(value, rows - 1, 0), 0.0)

    face = 0.5 * strength * (q_last + following(q_first))
    scale = face / (1.0 + face * (last_reach + following(first_reach)))
    below = jnp.where(row > 0, scale * cross_reach, 0.0)
    above = scale * following(cross_reach)
    flux = scale * (last_part - following(first_part))
    step = 1
    while step < rows:
        below_low, above_low, flux_low = (pltpu.roll(v, step, 0) for v in (below, above, flux))
        below_high, above_high, flux_high = (
            pltpu.roll(v, rows - step, 0) for v in (below, above, flux)
        )
        inverse = 1.0 / (1.0 - below * above_low - above * below_high)
        flux = (flux + below * flux_low + above * flux_high) * inverse
        below = below * below_low * inverse
        above = above * above_high * inverse
        step *= 2
    return jnp.where(row > 0, pltpu.roll(flux, 1, 0), 0.0), flux


def wide(pieces):
    return jnp.concatenate(pieces, axis=1)


def span_forward(layers, rows, warm, speed, energy, send, ratios, partials, reaches):
    opens = (lax.axis_index("gx") == 0).astype(jnp.float32)

    def coefficient_at(i):
        warmth = warm[pl.ds(i, layers, stride=rows), :]
        return wide([jnp.exp(slope * warmth) for slope in SLOPES])

    def source_at(i):
        where = pl.ds(i, layers, stride=rows)
        warmth = warm[where, :]
        return wide([warmth + energy[where, :], speed[where, :] + lifting_push * warmth])

    def keep(i, ratio, partial, reach):
        where = slice(i * layers, (i + 1) * layers)
        ratios[where, :] = ratio
        partials[where, :] = partial
        reaches[where, :] = reach

    values = block_sweep(rows, coefficient_at, source_at, span_strength, opens, keep)
    for number, value in enumerate(values):
        for pair in range(PAIRS):
            send[pl.ds(pair * layers * SENT + number, layers, stride=SENT), :] = value[
                :, pair * LANES : (pair + 1) * LANES
            ]


def span_reduced(blocks, received, fluxes):
    values = [received[pl.ds(number, blocks, stride=SENT), :] for number in range(CROSS_SENT)]
    low, high = interface_flux(values, span_strength, blocks)
    fluxes[pl.ds(0, blocks, stride=SIDES), :] = low
    fluxes[pl.ds(1, blocks, stride=SIDES), :] = high


def span_back_cross_forward(
    layers, rows, breadth, warm, flux, ratios, partials, reaches,
    send, cross_ratios, cross_partials, cross_reaches, solved, turned, turned_warm,
):
    halves = breadth // LANES
    lines = layers * rows
    group = min(LANES, lines)
    groups = lines // group
    length = breadth // CHUNKS
    for h in range(halves):
        across = slice(h * LANES, (h + 1) * LANES)
        for g in range(groups):
            turned_warm[g * breadth + h * LANES : g * breadth + (h + 1) * LANES, :] = warm[
                g * group : (g + 1) * group, across
            ].T
    for h in range(halves):
        low, high = (
            wide([
                flux[pl.ds((h * PAIRS + pair) * layers * SIDES + side, layers, stride=SIDES), :]
                for pair in range(PAIRS)
            ])
            for side in range(SIDES)
        )

        def kept_at(i):
            where = slice((h * rows + i) * layers, (h * rows + i + 1) * layers)
            return ratios[where, :], partials[where, :], reaches[where, :]

        def give(i, answer):
            for pair in range(PAIRS):
                start = (h * PAIRS + pair) * lines + i
                solved[pl.ds(start, layers, stride=rows), :] = answer[
                    :, pair * LANES : (pair + 1) * LANES
                ]

        block_return(rows, kept_at, low, high, give)
        for pair in range(PAIRS):
            for g in range(groups):
                start = (h * PAIRS + pair) * lines + g * group
                target = (pair * groups + g) * breadth + h * LANES
                turned[target : target + LANES, :] = solved[start : start + group, :].T

    def chunk_row(ref, number, t):
        return ref[pl.ds(number * breadth + t, CHUNKS, stride=length), :]

    def coefficient_at(t):
        warmth = [chunk_row(turned_warm, g, t) for g in range(groups)]
        return wide([jnp.exp(slope * w) for slope in SLOPES for w in warmth])

    def source_at(t):
        return wide([chunk_row(turned, number, t) for number in range(PAIRS * groups)])

    def keep(t, ratio, partial, reach):
        where = slice(t * CHUNKS, (t + 1) * CHUNKS)
        cross_ratios[where, :] = ratio
        cross_partials[where, :] = partial
        cross_reaches[where, :] = reach

    leading = lax.broadcasted_iota(jnp.int32, (CHUNKS, PAIRS * lines), 0) == 0
    opens = jnp.where(leading, (lax.axis_index("gy") == 0).astype(jnp.float32), 0.0)
    values = block_sweep(length, coefficient_at, source_at, cross_strength, opens, keep)
    for number, value in enumerate(values):
        send[number * CHUNKS : (number + 1) * CHUNKS, :] = value


def cross_back_depth(
    layers, rows, breadth, parts, warm, received, ratios, partials, reaches,
    new_warmth, new_speed, fluxes, turned, solved, depth_ratios, depth_partials,
):
    halves = breadth // LANES
    lines = layers * rows
    group = min(LANES, lines)
    groups = lines // group
    length = breadth // CHUNKS
    own = lax.axis_index("gy")
    for pair in range(PAIRS):
        span = slice(pair * lines, (pair + 1) * lines)
        values = []
        for number in range(CROSS_SENT):
            starts = [(d * CROSS_SENT + number) * CHUNKS for d in range(parts)]
            pieces = [received[start : start + CHUNKS, span] for start in starts]
            values.append(jnp.concatenate(pieces, axis=0))
        low, high = interface_flux(values, cross_strength, parts * CHUNKS)
        fluxes[0 : parts * CHUNKS, span] = low
        fluxes[parts * CHUNKS :, span] = high
    low = fluxes[pl.ds(pl.multiple_of(own * CHUNKS, CHUNKS), CHUNKS), :]
    high = fluxes[pl.ds(pl.multiple_of((parts + own) * CHUNKS, CHUNKS), CHUNKS), :]

    def kept_at(t):
        where = slice(t * CHUNKS, (t + 1) * CHUNKS)
        return ratios[where, :], partials[where, :], reaches[where, :]

    def give(t, answer):
        for number in range(PAIRS * groups):
            turned[pl.ds(number * breadth + t, CHUNKS, stride=length), :] = answer[
                :, number * group : (number + 1) * group
            ]

    block_return(length, kept_at, low, high, give)
    for number in range(PAIRS * groups):
        for h in range(halves):
            start = number * breadth + h * LANES
            solved[number * group : (number + 1) * group, h * LANES : (h + 1) * LANES] = turned[
                start : start + LANES, :
            ].T
    for pair, out in enumerate((new_warmth, new_speed)):
        half = 0.5 * depth_strength

        def coefficient_at(z):
            return jnp.exp(SLOPES[pair] * warm[z * rows : (z + 1) * rows, :])

        def source_at(z):
            return solved[pair * lines + z * rows : pair * lines + (z + 1) * rows, :]

        q_now = coefficient_at(0)
        numerator = source_at(0)
        delta = 1.0 + half * q_now
        for z in range(layers - 1):
            where = slice(z * rows, (z + 1) * rows)
            q_next = coefficient_at(z + 1)
            face = half * (q_now + q_next)
            inverse = 1.0 / (delta + face)
            ratio = face * inverse
            partial = numerator * inverse
            depth_ratios[where, :] = ratio
            depth_partials[where, :] = partial
            delta = 1.0 + delta * ratio
            numerator = source_at(z + 1) + face * partial
            q_now = q_next
        answer = numerator / (delta + half * q_now)
        out[(layers - 1) * rows : layers * rows, :] = answer
        for z in reversed(range(layers - 1)):
            where = slice(z * rows, (z + 1) * rows)
            answer = depth_partials[where, :] + depth_ratios[where, :] * answer
            out[where, :] = answer


def shaped(*shape):
    return jax.ShapeDtypeStruct(shape, jnp.float32)


def held(*shape):
    return pltpu.VMEM(shape, jnp.float32)


INTERPRET = False


def body(prior_warmth, prior_speed, energy_input):
    layers, rows, breadth = prior_warmth.shape
    lines = layers * rows
    halves = breadth // LANES
    group = min(LANES, lines)
    blocks = lax.axis_size("gx")
    parts = lax.axis_size("gy")
    warm, speed, energy = (v.reshape(lines, breadth) for v in (prior_warmth, prior_speed, energy_input))
    kept = shaped(halves * lines, PAIRS * LANES)
    column_spec = pl.BlockSpec((lines, LANES), lambda h: (0, h))
    kept_spec = pl.BlockSpec((lines, PAIRS * LANES), lambda h: (h, 0))
    send_rows = PAIRS * layers * SENT
    send, ratios, partials, reaches = pl.pallas_call(
        functools.partial(span_forward, layers, rows),
        grid=(halves,),
        in_specs=[column_spec] * 3,
        out_specs=(pl.BlockSpec((send_rows, LANES), lambda h: (h, 0)), kept_spec, kept_spec, kept_spec),
        out_shape=(shaped(blocks * SENT, LANES), kept, kept, kept),
        name="span_forward",
        interpret=INTERPRET,
    )(warm, speed, energy)
    received = lax.all_to_all(
        send.reshape(blocks, SENT, LANES), "gx", split_axis=0, concat_axis=0, tiled=True
    )
    flux = pl.pallas_call(
        functools.partial(span_reduced, blocks),
        out_shape=shaped(blocks * SIDES, LANES),
        name="span_reduced",
        interpret=INTERPRET,
    )(received.reshape(blocks * SENT, LANES))
    flux = lax.all_to_all(
        flux.reshape(blocks, SIDES, LANES), "gx", split_axis=0, concat_axis=0, tiled=True
    ).reshape(blocks * SIDES, LANES)
    kept = shaped(breadth, PAIRS * lines)
    send, cross_ratios, cross_partials, cross_reaches = pl.pallas_call(
        functools.partial(span_back_cross_forward, layers, rows, breadth),
        out_shape=(shaped(CROSS_SENT * CHUNKS, PAIRS * lines), kept, kept, kept),
        scratch_shapes=[
            held(halves * PAIRS * lines, LANES),
            held(PAIRS * lines // group * breadth, group),
            held(lines // group * breadth, group),
        ],
        name="span_back_cross_forward",
        interpret=INTERPRET,
    )(warm, flux, ratios, partials, reaches)
    spread = jnp.broadcast_to(send[None], (parts,) + send.shape)
    gathered = lax.all_to_all(spread, "gy", split_axis=0, concat_axis=0, tiled=True)
    out = shaped(lines, breadth)
    finished = pl.pallas_call(
        functools.partial(cross_back_depth, layers, rows, breadth, parts),
        out_shape=(out, out),
        scratch_shapes=[
            held(2 * parts * CHUNKS, PAIRS * lines),
            held(PAIRS * lines // group * breadth, group),
            held(PAIRS * lines, breadth),
            held(lines, breadth),
            held(lines, breadth),
        ],
        name="cross_back_depth",
        interpret=INTERPRET,
    )(
        warm, gathered.reshape(parts * CROSS_SENT * CHUNKS, PAIRS * lines),
        cross_ratios, cross_partials, cross_reaches,
    )
    return tuple(v.reshape(layers, rows, breadth) for v in finished)


def solution(mesh):
    in_specs = (P(None, "gx", "gy"), P(None, "gx", "gy"), P(None, "gx", "gy"))
    out_specs = (P(None, "gx", "gy"), P(None, "gx", "gy"))
    return jax.shard_map(body, mesh=mesh, in_specs=in_specs, out_specs=out_specs, check_vma=False)
```

profile of v0, /device:TPU:1, one launch (start us, length us, event | category | flops | bytes accessed | tf_op | source)
XLA Modules:
  0.0 66.4 jit_solution(10283025882282231682)
XLA Ops:
  0.6 2.5 %span_forward.1 = (f32[512,128]{1,0:T(8,128)}, f32[512,256]{1,0:T(8,128)}, f32[512,256]{1,0:T(8,128)}, f32[512,256]{1,0:T(8,128)}) custom-call(f32[256,256]{1,0:T(8,128)} %bitcast.10, f32[256,256]{1,0:T(8,128)} %bitcast.15, f32[256,256]{1,0:T(8,128)} %bitcast.16), custom_call_target="tpu_custom_call" | custom-call | tf_op jit(solution)/shard_map/span_forward/pallas_call | solution.py:290
  3.2 26.3 %all_to_all.15 = f32[64,8,128]{2,1,0:T(8,128)} all-to-all(f32[64,8,128]{2,1,0:T(8,128)} %bitcast.18), channel_id=1, replica_groups=mesh['gx'=64,'gy'=4] {'gx'}, dimensions={0} | all-to-all | bytes 524288 | tf_op jit(solution)/shard_map/all_to_all | solution.py:299
  29.4 1.8 %span_reduced.1 = f32[128,128]{1,0:T(8,128)} custom-call(f32[512,128]{1,0:T(8,128)} %bitcast.14), custom_call_target="tpu_custom_call" | custom-call | tf_op jit(solution)/shard_map/span_reduced/pallas_call | solution.py:302
  31.2 15.1 %all_to_all.16 = f32[64,2,128]{2,1,0:T(2,128)} all-to-all(f32[64,2,128]{2,1,0:T(2,128)} %bitcast.17), channel_id=1, replica_groups=mesh['gx'=64,'gy'=4] {'gx'}, dimensions={0} | all-to-all | bytes 131072 | tf_op jit(solution)/shard_map/all_to_all | solution.py:308
  46.3 3.7 %span_back_cross_forward.1 = (f32[56,512]{1,0:T(8,128)}, f32[256,512]{1,0:T(8,128)}, f32[256,512]{1,0:T(8,128)}, f32[256,512]{1,0:T(8,128)}) custom-call(f32[256,256]{1,0:T(8,128)} %bitcast.11, f32[128,128]{1,0:T(8,128)} %bitcast.19, f32[512,256]{1,0:T(8,128)} %get-tuple-element.13.ratios, f32[512,256]{1,0:T(8,128)} %get-tuple-element.14.partials, ...), custom_call_target="tpu_custom_call" | custom-call | tf_op jit(solution)/shard_map/span_back_cross_forward/pallas_call | solution.py:312
  50.0 0.9 %broadcast_in_dim.2 = f32[4,56,512]{2,1,0:T(8,128)S(1)} broadcast(f32[56,512]{1,0:T(8,128)} %get-tuple-element.16), dimensions={1,2} | broadcast | bytes 573440 | tf_op jit(solution)/shard_map/broadcast_in_dim | solution.py:323
  50.9 12.3 %all_to_all.17 = f32[4,56,512]{2,1,0:T(8,128)} all-to-all(f32[4,56,512]{2,1,0:T(8,128)S(1)} %broadcast_in_dim.2), channel_id=1, replica_groups=mesh['gx'=64,'gy'=4] {'gy'}, dimensions={0} | all-to-all | bytes 917504 | tf_op jit(solution)/shard_map/all_to_all | solution.py:324
  63.2 3.2 %cross_back_depth.1 = (f32[256,256]{1,0:T(8,128)}, f32[256,256]{1,0:T(8,128)}) custom-call(f32[256,256]{1,0:T(8,128)} %bitcast.12, f32[224,512]{1,0:T(8,128)} %bitcast.13, f32[256,512]{1,0:T(8,128)} %get-tuple-element.17.ratios, f32[256,512]{1,0:T(8,128)} %get-tuple-element.18.partials, f32[256,512]{1,0:T(8,128)} %get-tuple-element.19.reaches), custom_call_target="tpu_custom_call" | custom-call | tf_op jit(solution)/shard_map/cross_back_depth/pallas_call | solution.py:326
where the time goes:
time: 66.8 us; the launch traced here: 66.4 us
  blocking collectives  53.6 us (80%)
  Pallas kernels  11.2 us (17%)
  local copies, waits for them, and re-layouts  0.94 us (1%)
    all_to_all x1, blocking collectives, body(): lax.all_to_all(send.reshape(blocks, SENT, LANES), 'gx', split_axis=0, con...  26.3 us
    all_to_all x1, blocking collectives, body(): lax.all_to_all(flux.reshape(blocks, SIDES, LANES), 'gx', split_axis=0, co...  15.1 us
    all_to_all x1, blocking collectives, body(): lax.all_to_all(spread, 'gy', split_axis=0, concat_axis=0, tiled=True)  12.3 us
    pallas_call x1, Pallas kernels, body(): pl.pallas_call(functools.partial(span_back_cross_forward, layers, rows, b...  3.69 us
    pallas_call x1, Pallas kernels, body(): pl.pallas_call(functools.partial(cross_back_depth, layers, rows, breadth,...  3.22 us
    pallas_call x1, Pallas kernels, body(): pl.pallas_call(functools.partial(span_forward, layers, rows), grid=(halve...  2.55 us
    pallas_call x1, Pallas kernels, body(): pl.pallas_call(functools.partial(span_reduced, blocks), out_shape=shaped(...  1.77 us

commit v1 on v0

--- a/solution.py
+++ b/solution.py
@@ -90,6 +90,82 @@
     return jnp.where(row > 0, pltpu.roll(flux, 1, 0), 0.0), flux
 
 
+def merge_chunks(values, strength, rows):
+    first_part, last_part, first_reach, cross_reach, last_reach, q_first, q_last = values
+    row = lax.broadcasted_iota(jnp.int32, first_part.shape, 0)
+
+    def following(value):
+        return pltpu.roll(value, rows - 1, 0)
+
+    def preceding(value):
+        return pltpu.roll(value, 1, 0)
+
+    face = 0.5 * strength * (q_last + following(q_first))
+    scale = face / (1.0 + face * (last_reach + following(first_reach)))
+    scale = jnp.where(row < rows - 1, scale, 0.0)
+    below = scale * cross_reach
+    above = scale * following(cross_reach)
+    fixed = scale * (last_part - following(first_part))
+    by_low = jnp.where(row == 0, below, 0.0)
+    by_high = jnp.where(row == rows - 2, above, 0.0)
+    below = jnp.where(row > 0, below, 0.0)
+    above = jnp.where(row < rows - 2, above, 0.0)
+    step = 1
+    while step < rows:
+        lows = [pltpu.roll(v, step, 0) for v in (below, above, fixed, by_low, by_high)]
+        highs = [pltpu.roll(v, rows - step, 0) for v in (below, above, fixed, by_low, by_high)]
+        inverse = 1.0 / (1.0 - below * lows[1] - above * highs[0])
+        fixed, by_low, by_high = (
+            (now + below * low + above * high) * inverse
+            for now, low, high in zip((fixed, by_low, by_high), lows[2:], highs[2:])
+        )
+        below = below * lows[0] * inverse
+        above = above * highs[1] * inverse
+        step *= 2
+    by_high = jnp.where(row < rows - 1, by_high, 1.0)
+    merged = (
+        (first_part - cross_reach * fixed, 0),
+        (last_part + cross_reach * preceding(fixed), rows - 1),
+        (first_reach - cross_reach * by_low, 0),
+        (cross_reach * preceding(by_low), rows - 1),
+        (last_reach - cross_reach * preceding(by_high), rows - 1),
+        (q_first, 0),
+        (q_last, rows - 1),
+    )
+    return (fixed, by_low, by_high), [value[at : at + 1, :] for value, at in merged]
+
+
+def own_flux(parts_values, strength, own):
+    half = 0.5 * strength
+    ratios, fluxes = [], []
+    for j, (_, last_part, _, cross_reach, last_reach, _, q_last) in enumerate(parts_values):
+        if j + 1 < len(parts_values):
+            first_part, _, first_reach, next_cross, _, q_first, _ = parts_values[j + 1]
+            face = half * (q_last + q_first)
+            centre = 1.0 + face * (last_reach + first_reach)
+            right = face * (last_part - first_part)
+            above = face * next_cross
+        else:
+            face = half * q_last
+            centre = 1.0 + face * last_reach
+            right = face * last_part
+            above = None
+        if j:
+            below = face * cross_reach
+            centre = centre - below * ratios[-1]
+            right = right + below * fluxes[-1]
+        inverse = 1.0 / centre
+        fluxes.append(right * inverse)
+        ratios.append(None if above is None else above * inverse)
+    high = flux = fluxes[-1]
+    low = jnp.zeros_like(flux)
+    for j in reversed(range(len(fluxes) - 1)):
+        flux = fluxes[j] + ratios[j] * flux
+        low = jnp.where(own == j + 1, flux, low)
+        high = jnp.where(own == j, flux, high)
+    return low, high
+
+
 def wide(pieces):
     return jnp.concatenate(pieces, axis=1)
 
@@ -129,7 +205,7 @@
 
 def span_back_cross_forward(
     layers, rows, breadth, warm, flux, ratios, partials, reaches,
-    send, cross_ratios, cross_partials, cross_reaches, solved, turned, turned_warm,
+    send, chunk_fluxes, cross_ratios, cross_partials, cross_reaches, solved, turned, turned_warm,
 ):
     halves = breadth // LANES
     lines = layers * rows
@@ -188,32 +264,39 @@
     leading = lax.broadcasted_iota(jnp.int32, (CHUNKS, PAIRS * lines), 0) == 0
     opens = jnp.where(leading, (lax.axis_index("gy") == 0).astype(jnp.float32), 0.0)
     values = block_sweep(length, coefficient_at, source_at, cross_strength, opens, keep)
-    for number, value in enumerate(values):
-        send[number * CHUNKS : (number + 1) * CHUNKS, :] = value
+    linear, merged = merge_chunks(values, cross_strength, CHUNKS)
+    for number, value in enumerate(linear):
+        chunk_fluxes[number * CHUNKS : (number + 1) * CHUNKS, :] = value
+    for number, value in enumerate(merged + merged[-1:]):
+        send[number : number + 1, :] = value
 
 
 def cross_back_depth(
-    layers, rows, breadth, parts, warm, received, ratios, partials, reaches,
-    new_warmth, new_speed, fluxes, turned, solved, depth_ratios, depth_partials,
+    layers, rows, breadth, parts, warm, *refs
 ):
+    received, refs = refs[:parts], refs[parts:]
+    chunk_fluxes, ratios, partials, reaches, new_warmth, new_speed = refs[:6]
+    ordered, turned, solved, depth_ratios, depth_partials = refs[6:]
     halves = breadth // LANES
     lines = layers * rows
     group = min(LANES, lines)
     groups = lines // group
     length = breadth // CHUNKS
     own = lax.axis_index("gy")
-    for pair in range(PAIRS):
-        span = slice(pair * lines, (pair + 1) * lines)
-        values = []
-        for number in range(CROSS_SENT):
-            starts = [(d * CROSS_SENT + number) * CHUNKS for d in range(parts)]
-            pieces = [received[start : start + CHUNKS, span] for start in starts]
-            values.append(jnp.concatenate(pieces, axis=0))
-        low, high = interface_flux(values, cross_strength, parts * CHUNKS)
-        fluxes[0 : parts * CHUNKS, span] = low
-        fluxes[parts * CHUNKS :, span] = high
-    low = fluxes[pl.ds(pl.multiple_of(own * CHUNKS, CHUNKS), CHUNKS), :]
-    high = fluxes[pl.ds(pl.multiple_of((parts + own) * CHUNKS, CHUNKS), CHUNKS), :]
+    for steps in range(parts):
+        slot = lax.rem(own + parts - steps, parts)
+        ordered[pl.ds(pl.multiple_of(slot * SENT, SENT), SENT), :] = received[steps][...]
+    parts_values = [
+        [ordered[d * SENT + number : d * SENT + number + 1, :] for number in range(CROSS_SENT)]
+        for d in range(parts)
+    ]
+    end_low, end_high = own_flux(parts_values, cross_strength, own)
+    fixed, by_low, by_high = (
+        chunk_fluxes[number * CHUNKS : (number + 1) * CHUNKS, :] for number in range(3)
+    )
+    high = fixed + by_low * end_low + by_high * end_high
+    row = lax.broadcasted_iota(jnp.int32, high.shape, 0)
+    low = jnp.where(row > 0, pltpu.roll(high, 1, 0), end_low)
 
     def kept_at(t):
         where = slice(t * CHUNKS, (t + 1) * CHUNKS)
@@ -309,9 +392,11 @@
         flux.reshape(blocks, SIDES, LANES), "gx", split_axis=0, concat_axis=0, tiled=True
     ).reshape(blocks * SIDES, LANES)
     kept = shaped(breadth, PAIRS * lines)
-    send, cross_ratios, cross_partials, cross_reaches = pl.pallas_call(
+    send, chunk_fluxes, *cross_kept = pl.pallas_call(
         functools.partial(span_back_cross_forward, layers, rows, breadth),
-        out_shape=(shaped(CROSS_SENT * CHUNKS, PAIRS * lines), kept, kept, kept),
+        out_shape=(
+            shaped(SENT, PAIRS * lines), shaped(3 * CHUNKS, PAIRS * lines), kept, kept, kept,
+        ),
         scratch_shapes=[
             held(halves * PAIRS * lines, LANES),
             held(PAIRS * lines // group * breadth, group),
@@ -320,14 +405,16 @@
         name="span_back_cross_forward",
         interpret=INTERPRET,
     )(warm, flux, ratios, partials, reaches)
-    spread = jnp.broadcast_to(send[None], (parts,) + send.shape)
-    gathered = lax.all_to_all(spread, "gy", split_axis=0, concat_axis=0, tiled=True)
+    received = [send] + [
+        lax.ppermute(send, "gy", [(i, (i + steps) % parts) for i in range(parts)])
+        for steps in range(1, parts)
+    ]
     out = shaped(lines, breadth)
     finished = pl.pallas_call(
         functools.partial(cross_back_depth, layers, rows, breadth, parts),
         out_shape=(out, out),
         scratch_shapes=[
-            held(2 * parts * CHUNKS, PAIRS * lines),
+            held(parts * SENT, PAIRS * lines),
             held(PAIRS * lines // group * breadth, group),
             held(PAIRS * lines, breadth),
             held(lines, breadth),
@@ -335,10 +422,7 @@
         ],
         name="cross_back_depth",
         interpret=INTERPRET,
-    )(
-        warm, gathered.reshape(parts * CROSS_SENT * CHUNKS, PAIRS * lines),
-        cross_ratios, cross_partials, cross_reaches,
-    )
+    )(warm, *received, chunk_fluxes, *cross_kept)
     return tuple(v.reshape(layers, rows, breadth) for v in finished)
 
 

time: 66.8 us -> 61.1 us (0.915)
  blocking collectives: 53.6 us -> 41.4 us
  starting transfers between devices: 0 us -> 3.77 us
  waiting for transfers between devices: 0 us -> 3.43 us
    all_to_all x1 -> x0, blocking collectives: 12.3 us -> none  [body(): lax.all_to_all(spread, 'gy', split_axis=0, concat_axis=0, tiled=True)]
    ppermute x0 -> x3, starting transfers between devices: none -> 3.77 us  [body(): lax.ppermute(send, 'gy', [(i, (i + steps) % parts) for i in range(parts)])]
    ppermute x0 -> x3, waiting for transfers between devices: none -> 3.43 us  [body(): lax.ppermute(send, 'gy', [(i, (i + steps) % parts) for i in range(parts)])]
    broadcast_in_dim x1 -> x0, local copies, waits for them, and re-layouts: 0.94 us -> none  [body(): spread = jnp.broadcast_to(send[None], (parts,) + send.shape)]
  transfers between devices with their start and end apart: 0 -> 3, of which waited for: 0 -> 2; matrix products, arithmetic and copies ran while one was open for 0% -> 0% of each run, Pallas kernels for 0% -> 0%
where the time goes in v1:
time: 61.1 us; the launch traced here: 60.8 us
  blocking collectives  41.4 us (68%)
  Pallas kernels  11 us (18%)
  starting transfers between devices  3.77 us (6%)
  waiting for transfers between devices  3.43 us (6%)
  between operations  0.64 us (1%)
    all_to_all x1, blocking collectives, body(): lax.all_to_all(send.reshape(blocks, SENT, LANES), 'gx', split_axis=0, con...  26.3 us
    all_to_all x1, blocking collectives, body(): lax.all_to_all(flux.reshape(blocks, SIDES, LANES), 'gx', split_axis=0, co...  15.1 us
    ppermute x3, starting transfers between devices, body(): lax.ppermute(send, 'gy', [(i, (i + steps) % parts) for i in range(parts)])  3.77 us
    pallas_call x1, Pallas kernels, body(): pl.pallas_call(functools.partial(span_back_cross_forward, layers, rows, b...  3.69 us
    ppermute x3, waiting for transfers between devices, body(): lax.ppermute(send, 'gy', [(i, (i + steps) % parts) for i in range(parts)])  3.43 us
    pallas_call x1, Pallas kernels, body(): pl.pallas_call(functools.partial(cross_back_depth, layers, rows, breadth,...  2.95 us
    pallas_call x1, Pallas kernels, body(): pl.pallas_call(functools.partial(span_forward, layers, rows), grid=(halve...  2.55 us
    pallas_call x1, Pallas kernels, body(): pl.pallas_call(functools.partial(span_reduced, blocks), out_shape=shaped(...  1.77 us
  transfers between devices with their start and end apart: 3, of which 2 were waited for; matrix products, arithmetic and copies ran while one was open for 0% of the time, Pallas kernels for 0%

profile of v1, /device:TPU:1, one launch (start us, length us, event | category | flops | bytes accessed | tf_op | source)
XLA Modules:
  0.0 60.8 jit_solution(16013511720741128202)
XLA Ops:
  0.6 2.5 %span_forward.1 = (f32[512,128]{1,0:T(8,128)}, f32[512,256]{1,0:T(8,128)}, f32[512,256]{1,0:T(8,128)}, f32[512,256]{1,0:T(8,128)}) custom-call(f32[256,256]{1,0:T(8,128)} %bitcast.9, f32[256,256]{1,0:T(8,128)} %bitcast.13, f32[256,256]{1,0:T(8,128)} %bitcast.14), custom_call_target="tpu_custom_call" | custom-call | tf_op jit(solution)/shard_map/span_forward/pallas_call | solution.py:373
  3.2 26.3 %all_to_all.10 = f32[64,8,128]{2,1,0:T(8,128)} all-to-all(f32[64,8,128]{2,1,0:T(8,128)} %bitcast.16), channel_id=1, replica_groups=mesh['gx'=64,'gy'=4] {'gx'}, dimensions={0} | all-to-all | bytes 524288 | tf_op jit(solution)/shard_map/all_to_all | solution.py:382
  29.4 1.8 %span_reduced.1 = f32[128,128]{1,0:T(8,128)} custom-call(f32[512,128]{1,0:T(8,128)} %bitcast.12), custom_call_target="tpu_custom_call" | custom-call | tf_op jit(solution)/shard_map/span_reduced/pallas_call | solution.py:385
  31.2 15.1 %all_to_all.11 = f32[64,2,128]{2,1,0:T(2,128)} all-to-all(f32[64,2,128]{2,1,0:T(2,128)} %bitcast.15), channel_id=1, replica_groups=mesh['gx'=64,'gy'=4] {'gx'}, dimensions={0} | all-to-all | bytes 131072 | tf_op jit(solution)/shard_map/all_to_all | solution.py:391
  46.3 3.7 %span_back_cross_forward.1 = (f32[8,512]{1,0:T(8,128)}, f32[24,512]{1,0:T(8,128)}, f32[256,512]{1,0:T(8,128)}, f32[256,512]{1,0:T(8,128)}, f32[256,512]{1,0:T(8,128)}) custom-call(f32[256,256]{1,0:T(8,128)} %bitcast.10, f32[128,128]{1,0:T(8,128)} %bitcast.17, f32[512,256]{1,0:T(8,128)} %get-tuple-element.14.ratios, f32[512,256]{1,0:T(8,128)} %get-tuple-element.15.partials, ...), custom_call_target="tpu_custom_call" | custom-call | tf_op jit(solution)/shard_map/span_back_cross_forward/pallas_call | solution.py:395
  50.0 2.7 %collective-permute-start.2 = (f32[8,512]{1,0:T(8,128)}, f32[8,512]{1,0:T(8,128)S(1)}, u32[]{:S(2)}, u32[]{:S(2)}) collective-permute-start(f32[8,512]{1,0:T(8,128)} %get-tuple-element.17.refs_0_), channel_id=1, source_target_pairs={{0,3},{1,0},{2,1},{3,2},{4,7},{5,4},{6,5},{7,6},{8,11},{9,8},{10,9... | collective-permute-start | bytes 49160 | tf_op jit(solution)/shard_map/ppermute | solution.py:409
  52.8 0.3 collective-permute-start.1
  53.1 0.7 %collective-permute-start = (f32[8,512]{1,0:T(8,128)}, f32[8,512]{1,0:T(8,128)S(1)}, u32[]{:S(2)}, u32[]{:S(2)}) collective-permute-start(f32[8,512]{1,0:T(8,128)} %get-tuple-element.17.refs_0_), channel_id=1, source_target_pairs={{0,1},{1,2},{2,3},{3,0},{4,5},{5,6},{6,7},{7,4},{8,9},{9,10},{10,1... | collective-permute-start | bytes 49160 | tf_op jit(solution)/shard_map/ppermute | solution.py:409
  53.8 0.0 collective-permute-done.2.refs_3_
  53.8 0.0 copy-start
  53.8 3.2 %collective-permute-done.1.refs_2_ = f32[8,512]{1,0:T(8,128)S(1)} collective-permute-done((f32[8,512]{1,0:T(8,128)}, f32[8,512]{1,0:T(8,128)S(1)}, u32[]{:S(2)}, u32[]{:S(2)}) %collective-permute-start.1) | collective-permute-done | bytes 16416 | tf_op jit(solution)/shard_map/ppermute | solution.py:409
  57.1 0.0 copy-start.1
  57.1 0.2 collective-permute-done.refs_1_
  57.2 0.0 copy-start.2
  57.2 0.0 copy-done
  57.2 0.4 copy-done.1
  57.7 0.2 copy-done.2
  57.8 3.0 %cross_back_depth.1 = (f32[256,256]{1,0:T(8,128)}, f32[256,256]{1,0:T(8,128)}) custom-call(f32[256,256]{1,0:T(8,128)} %bitcast.11, f32[8,512]{1,0:T(8,128)} %get-tuple-element.17.refs_0_, f32[8,512]{1,0:T(8,128)} %copy-done.2, f32[8,512]{1,0:T(8,128)} %copy-done.1, f32[8,512]{1,0:T(8,128)} %copy-done, f32[24,512]{1,0:T(8,128)} %get-tuple-element.18.refs_4_, ...), custom_call_target="tpu_custom_call" | custom-call | tf_op jit(solution)/shard_map/cross_back_depth/pallas_call | solution.py:413
Async XLA Ops:
  50.0 3.8 %collective-permute-start.2 = (f32[8,512]{1,0:T(8,128)}, f32[8,512]{1,0:T(8,128)S(1)}, u32[]{:S(2)}, u32[]{:S(2)}) collective-permute-start(f32[8,512]{1,0:T(8,128)} %get-tuple-element.17.refs_0_), channel_id=1, source_target_pairs={{0,3},{1,0},{2,1},{3,2},{4,7},{5,4},{6,5},{7,6},{8,11},{9,8},{10,9... | collective-permute-start | bytes 49160 | tf_op jit(solution)/shard_map/ppermute | solution.py:409
  52.8 4.3 %collective-permute-start.1 = (f32[8,512]{1,0:T(8,128)}, f32[8,512]{1,0:T(8,128)S(1)}, u32[]{:S(2)}, u32[]{:S(2)}) collective-permute-start(f32[8,512]{1,0:T(8,128)} %get-tuple-element.17.refs_0_), channel_id=1, source_target_pairs={{0,2},{1,3},{2,0},{3,1},{4,6},{5,7},{6,4},{7,5},{8,10},{9,11},{10,... | collective-permute-start | bytes 49160 | tf_op jit(solution)/shard_map/ppermute | solution.py:409
  53.1 4.1 %collective-permute-start = (f32[8,512]{1,0:T(8,128)}, f32[8,512]{1,0:T(8,128)S(1)}, u32[]{:S(2)}, u32[]{:S(2)}) collective-permute-start(f32[8,512]{1,0:T(8,128)} %get-tuple-element.17.refs_0_), channel_id=1, source_target_pairs={{0,1},{1,2},{2,3},{3,0},{4,5},{5,6},{6,7},{7,4},{8,9},{9,10},{10,1... | collective-permute-start | bytes 49160 | tf_op jit(solution)/shard_map/ppermute | solution.py:409
  53.8 3.4 %copy-start = (f32[8,512]{1,0:T(8,128)}, f32[8,512]{1,0:T(8,128)S(1)}, u32[]{:S(2)}) copy-start(f32[8,512]{1,0:T(8,128)S(1)} %collective-permute-done.2.refs_3_) | copy-start | bytes 49156
  57.1 0.6 copy-start.1
  57.2 0.6 copy-start.2

commit v2 on v1

--- a/solution.py
+++ b/solution.py
@@ -20,6 +20,7 @@
 CHUNKS = 8
 SENT = 8
 SIDES = 2
+ROOM = 24 * 2**20
 CROSS_SENT = 7
 
 
@@ -183,7 +184,7 @@
         return wide([warmth + energy[where, :], speed[where, :] + lifting_push * warmth])
 
     def keep(i, ratio, partial, reach):
-        where = slice(i * layers, (i + 1) * layers)
+        where = pl.ds(pl.multiple_of((pl.program_id(0) * rows + i) * layers, layers), layers)
         ratios[where, :] = ratio
         partials[where, :] = partial
         reaches[where, :] = reach
@@ -355,6 +356,14 @@
     return pltpu.VMEM(shape, jnp.float32)
 
 
+def passed(*shape):
+    return pltpu.VMEM(shape, jnp.float32)
+
+
+def near(*values):
+    return [pltpu.with_memory_space_constraint(value, pltpu.VMEM) for value in values]
+
+
 INTERPRET = False
 
 
@@ -366,9 +375,9 @@
     blocks = lax.axis_size("gx")
     parts = lax.axis_size("gy")
     warm, speed, energy = (v.reshape(lines, breadth) for v in (prior_warmth, prior_speed, energy_input))
-    kept = shaped(halves * lines, PAIRS * LANES)
+    kept = passed(halves * lines, PAIRS * LANES)
     column_spec = pl.BlockSpec((lines, LANES), lambda h: (0, h))
-    kept_spec = pl.BlockSpec((lines, PAIRS * LANES), lambda h: (h, 0))
+    kept_spec = pl.BlockSpec(memory_space=pltpu.VMEM)
     send_rows = PAIRS * layers * SENT
     send, ratios, partials, reaches = pl.pallas_call(
         functools.partial(span_forward, layers, rows),
@@ -377,6 +386,7 @@
         out_specs=(pl.BlockSpec((send_rows, LANES), lambda h: (h, 0)), kept_spec, kept_spec, kept_spec),
         out_shape=(shaped(blocks * SENT, LANES), kept, kept, kept),
         name="span_forward",
+        compiler_params=pltpu.CompilerParams(vmem_limit_bytes=ROOM),
         interpret=INTERPRET,
     )(warm, speed, energy)
     received = lax.all_to_all(
@@ -384,18 +394,19 @@
     )
     flux = pl.pallas_call(
         functools.partial(span_reduced, blocks),
-        out_shape=shaped(blocks * SIDES, LANES),
+        out_shape=passed(blocks * SIDES, LANES),
         name="span_reduced",
+        compiler_params=pltpu.CompilerParams(vmem_limit_bytes=ROOM),
         interpret=INTERPRET,
-    )(received.reshape(blocks * SENT, LANES))
+    )(*near(received.reshape(blocks * SENT, LANES)))
     flux = lax.all_to_all(
         flux.reshape(blocks, SIDES, LANES), "gx", split_axis=0, concat_axis=0, tiled=True
     ).reshape(blocks * SIDES, LANES)
-    kept = shaped(breadth, PAIRS * lines)
+    kept = passed(breadth, PAIRS * lines)
     send, chunk_fluxes, *cross_kept = pl.pallas_call(
         functools.partial(span_back_cross_forward, layers, rows, breadth),
         out_shape=(
-            shaped(SENT, PAIRS * lines), shaped(3 * CHUNKS, PAIRS * lines), kept, kept, kept,
+            passed(SENT, PAIRS * lines), passed(3 * CHUNKS, PAIRS * lines), kept, kept, kept,
         ),
         scratch_shapes=[
             held(halves * PAIRS * lines, LANES),
@@ -403,8 +414,9 @@
             held(lines // group * breadth, group),
         ],
         name="span_back_cross_forward",
+        compiler_params=pltpu.CompilerParams(vmem_limit_bytes=ROOM),
         interpret=INTERPRET,
-    )(warm, flux, ratios, partials, reaches)
+    )(*near(warm, flux, ratios, partials, reaches))
     received = [send] + [
         lax.ppermute(send, "gy", [(i, (i + steps) % parts) for i in range(parts)])
         for steps in range(1, parts)
@@ -421,8 +433,9 @@
             held(lines, breadth),
         ],
         name="cross_back_depth",
+        compiler_params=pltpu.CompilerParams(vmem_limit_bytes=ROOM),
         interpret=INTERPRET,
-    )(warm, *received, chunk_fluxes, *cross_kept)
+    )(*near(warm, *received, chunk_fluxes, *cross_kept))
     return tuple(v.reshape(layers, rows, breadth) for v in finished)
 
 

time: 61.1 us -> 55 us (0.900)
  Pallas kernels: 11 us -> 3.56 us
  local copies, waits for them, and re-layouts: 0.6 us -> 2.85 us
  blocking collectives: 41.4 us -> 40.5 us
    pallas_call x1, Pallas kernels: 3.69 us -> 1.17 us  [body(): pl.pallas_call(functools.partial(span_back_cross_forward, layers, rows, b...]
    unnamed x6 -> x8, local copies, waits for them, and re-layouts: 0.6 us -> 2.85 us
    pallas_call x1, Pallas kernels: 2.55 us -> 0.78 us  [body(): pl.pallas_call(functools.partial(span_forward, layers, rows), grid=(halve...]
    pallas_call x1, Pallas kernels: 1.77 us -> 0.19 us  [body(): pl.pallas_call(functools.partial(span_reduced, blocks), out_shape=passed(...]
    pallas_call x1, Pallas kernels: 2.95 us -> 1.42 us  [body(): pl.pallas_call(functools.partial(cross_back_depth, layers, rows, breadth,...]
where the time goes in v2:
time: 55 us; the launch traced here: 54.7 us
  blocking collectives  40.5 us (74%)
  starting transfers between devices  3.85 us (7%)
  Pallas kernels  3.56 us (6%)
  waiting for transfers between devices  3.23 us (6%)
  local copies, waits for them, and re-layouts  2.85 us (5%)
  between operations  0.67 us (1%)
    all_to_all x1, blocking collectives, body(): lax.all_to_all(send.reshape(blocks, SENT, LANES), 'gx', split_axis=0, con...  25.9 us
    all_to_all x1, blocking collectives, body(): lax.all_to_all(flux.reshape(blocks, SIDES, LANES), 'gx', split_axis=0, co...  14.6 us
    ppermute x3, starting transfers between devices, body(): lax.ppermute(send, 'gy', [(i, (i + steps) % parts) for i in range(parts)])  3.85 us
    ppermute x3, waiting for transfers between devices, body(): lax.ppermute(send, 'gy', [(i, (i + steps) % parts) for i in range(parts)])  3.23 us
    unnamed x8, local copies, waits for them, and re-layouts  2.85 us
    pallas_call x1, Pallas kernels, body(): pl.pallas_call(functools.partial(cross_back_depth, layers, rows, breadth,...  1.42 us
    pallas_call x1, Pallas kernels, body(): pl.pallas_call(functools.partial(span_back_cross_forward, layers, rows, b...  1.17 us
  transfers between devices with their start and end apart: 3, of which 2 were waited for; matrix products, arithmetic and copies ran while one was open for 0% of the time, Pallas kernels for 0%

profile of v2, /device:TPU:1, one launch (start us, length us, event | category | flops | bytes accessed | tf_op | source)
XLA Modules:
  0.0 54.7 jit_solution(13039509690900766176)
XLA Ops:
  0.6 0.0 copy-start
  0.6 0.9 %copy-done = f32[16,16,256]{2,1,0:T(8,128)S(1)} copy-done((f32[16,16,256]{2,1,0:T(8,128)S(1)}, f32[16,16,256]{2,1,0:T(8,128)}, u32[]{:S(2)}) %copy-start) | copy-done | bytes 262168
  1.6 0.0 copy-start.2
  1.6 0.9 %copy-done.2 = f32[16,16,256]{2,1,0:T(8,128)S(1)} copy-done((f32[16,16,256]{2,1,0:T(8,128)S(1)}, f32[16,16,256]{2,1,0:T(8,128)}, u32[]{:S(2)}) %copy-start.2) | copy-done | bytes 262168
  2.5 0.0 copy-start.3
  2.5 0.9 %copy-done.3 = f32[16,16,256]{2,1,0:T(8,128)S(1)} copy-done((f32[16,16,256]{2,1,0:T(8,128)S(1)}, f32[16,16,256]{2,1,0:T(8,128)}, u32[]{:S(2)}) %copy-start.3) | copy-done | bytes 262168
  3.5 0.8 %span_forward.1 = (f32[512,128]{1,0:T(8,128)S(1)}, f32[512,256]{1,0:T(8,128)S(1)}, f32[512,256]{1,0:T(8,128)S(1)}, f32[512,256]{1,0:T(8,128)S(1)}) custom-call(f32[256,256]{1,0:T(8,128)S(1)} %bitcast.9, f32[256,256]{1,0:T(8,128)S(1)} %bitcast.13, f32[256,256]{1,0:T(8,128)S(1)} %bitcast.14), custom_call_target="tpu_custom_call" | custom-call | tf_op jit(solution)/shard_map/span_forward/pallas_call | solution.py:382
  4.3 25.9 %all_to_all.10 = f32[64,8,128]{2,1,0:T(8,128)S(1)} all-to-all(f32[64,8,128]{2,1,0:T(8,128)S(1)} %bitcast.16), channel_id=1, replica_groups=mesh['gx'=64,'gy'=4] {'gx'}, dimensions={0} | all-to-all | bytes 524288 | tf_op jit(solution)/shard_map/all_to_all | solution.py:392
  30.2 0.0 copy-start.1
  30.2 0.2 span_reduced.1
  30.4 14.6 %all_to_all.11 = f32[64,2,128]{2,1,0:T(2,128)S(1)} all-to-all(f32[64,2,128]{2,1,0:T(2,128)S(1)} %bitcast.15), channel_id=1, replica_groups=mesh['gx'=64,'gy'=4] {'gx'}, dimensions={0} | all-to-all | bytes 131072 | tf_op jit(solution)/shard_map/all_to_all | solution.py:402
  45.0 0.0 copy-done.1
  45.0 1.2 %span_back_cross_forward.1 = (f32[8,512]{1,0:T(8,128)S(1)}, f32[24,512]{1,0:T(8,128)S(1)}, f32[256,512]{1,0:T(8,128)S(1)}, f32[256,512]{1,0:T(8,128)S(1)}, f32[256,512]{1,0:T(8,128)S(1)}) custom-call(f32[256,256]{1,0:T(8,128)S(1)} %bitcast.10, f32[128,128]{1,0:T(8,128)S(1)} %bitcast.17, f32[512,256]{1,0:T(8,128)S(1)} %get-tuple-element.14.ratios, ...), custom_call_target="tpu_custom_call" | custom-call | tf_op jit(solution)/shard_map/span_back_cross_forward/pallas_call | solution.py:406
  46.2 2.8 %collective-permute-start.2 = (f32[8,512]{1,0:T(8,128)S(1)}, f32[8,512]{1,0:T(8,128)S(1)}, u32[]{:S(2)}, u32[]{:S(2)}) collective-permute-start(f32[8,512]{1,0:T(8,128)S(1)} %get-tuple-element.17.refs_0_), channel_id=1, source_target_pairs={{0,3},{1,0},{2,1},{3,2},{4,7},{5,4},{6,5},{7,6},{8,11},{9,8},{10,9... | collective-permute-start | bytes 49160 | tf_op jit(solution)/shard_map/ppermute | solution.py:421
  49.0 0.3 collective-permute-start.1
  49.4 0.7 %collective-permute-start = (f32[8,512]{1,0:T(8,128)S(1)}, f32[8,512]{1,0:T(8,128)S(1)}, u32[]{:S(2)}, u32[]{:S(2)}) collective-permute-start(f32[8,512]{1,0:T(8,128)S(1)} %get-tuple-element.17.refs_0_), channel_id=1, source_target_pairs={{0,1},{1,2},{2,3},{3,0},{4,5},{5,6},{6,7},{7,4},{8,9},{9,10},{10,1... | collective-permute-start | bytes 49160 | tf_op jit(solution)/shard_map/ppermute | solution.py:421
  50.1 0.0 collective-permute-done.2.refs_3_
  50.1 3.1 %collective-permute-done.1.refs_2_ = f32[8,512]{1,0:T(8,128)S(1)} collective-permute-done((f32[8,512]{1,0:T(8,128)S(1)}, f32[8,512]{1,0:T(8,128)S(1)}, u32[]{:S(2)}, u32[]{:S(2)}) %collective-permute-start.1) | collective-permute-done | bytes 16416 | tf_op jit(solution)/shard_map/ppermute | solution.py:421
  53.1 0.2 collective-permute-done.refs_1_
  53.3 1.4 %cross_back_depth.1 = (f32[256,256]{1,0:T(8,128)}, f32[256,256]{1,0:T(8,128)}) custom-call(f32[256,256]{1,0:T(8,128)S(1)} %bitcast.11, f32[8,512]{1,0:T(8,128)S(1)} %get-tuple-element.17.refs_0_, f32[8,512]{1,0:T(8,128)S(1)} %collective-permute-done.refs_1_, f32[8,512]{1,0:T(8,128)S(1)} %collective-permute-done.1.refs_2_, ...), custom_call_target="tpu_custom_call" | custom-call | tf_op jit(solution)/shard_map/cross_back_depth/pallas_call | solution.py:425
Async XLA Ops:
  0.6 1.0 %copy-start = (f32[16,16,256]{2,1,0:T(8,128)S(1)}, f32[16,16,256]{2,1,0:T(8,128)}, u32[]{:S(2)}) copy-start(f32[16,16,256]{2,1,0:T(8,128)} %param.3) | copy-start | bytes 786436
  1.6 0.9 %copy-start.2 = (f32[16,16,256]{2,1,0:T(8,128)S(1)}, f32[16,16,256]{2,1,0:T(8,128)}, u32[]{:S(2)}) copy-start(f32[16,16,256]{2,1,0:T(8,128)} %param.4) | copy-start | bytes 786436
  2.5 0.9 %copy-start.3 = (f32[16,16,256]{2,1,0:T(8,128)S(1)}, f32[16,16,256]{2,1,0:T(8,128)}, u32[]{:S(2)}) copy-start(f32[16,16,256]{2,1,0:T(8,128)} %param.5) | copy-start | bytes 786436
  30.2 14.8 %copy-start.1 = (f32[16,16,256]{2,1,0:T(8,128)S(1)}, f32[16,16,256]{2,1,0:T(8,128)}, u32[]{:S(2)}) copy-start(f32[16,16,256]{2,1,0:T(8,128)} %param.3) | copy-start | bytes 786436
  46.2 3.9 %collective-permute-start.2 = (f32[8,512]{1,0:T(8,128)S(1)}, f32[8,512]{1,0:T(8,128)S(1)}, u32[]{:S(2)}, u32[]{:S(2)}) collective-permute-start(f32[8,512]{1,0:T(8,128)S(1)} %get-tuple-element.17.refs_0_), channel_id=1, source_target_pairs={{0,3},{1,0},{2,1},{3,2},{4,7},{5,4},{6,5},{7,6},{8,11},{9,8},{10,9... | collective-permute-start | bytes 49160 | tf_op jit(solution)/shard_map/ppermute | solution.py:421
  49.0 4.1 %collective-permute-start.1 = (f32[8,512]{1,0:T(8,128)S(1)}, f32[8,512]{1,0:T(8,128)S(1)}, u32[]{:S(2)}, u32[]{:S(2)}) collective-permute-start(f32[8,512]{1,0:T(8,128)S(1)} %get-tuple-element.17.refs_0_), channel_id=1, source_target_pairs={{0,2},{1,3},{2,0},{3,1},{4,6},{5,7},{6,4},{7,5},{8,10},{9,11},{10,... | collective-permute-start | bytes 49160 | tf_op jit(solution)/shard_map/ppermute | solution.py:421
  49.4 3.9 %collective-permute-start = (f32[8,512]{1,0:T(8,128)S(1)}, f32[8,512]{1,0:T(8,128)S(1)}, u32[]{:S(2)}, u32[]{:S(2)}) collective-permute-start(f32[8,512]{1,0:T(8,128)S(1)} %get-tuple-element.17.refs_0_), channel_id=1, source_target_pairs={{0,1},{1,2},{2,3},{3,0},{4,5},{5,6},{6,7},{7,4},{8,9},{9,10},{10,1... | collective-permute-start | bytes 49160 | tf_op jit(solution)/shard_map/ppermute | solution.py:421

commit v3 on v2

--- a/solution.py
+++ b/solution.py
@@ -20,6 +20,7 @@
 CHUNKS = 8
 SENT = 8
 SIDES = 2
+PIECE = 4
 ROOM = 24 * 2**20
 CROSS_SENT = 7
 
@@ -171,30 +172,49 @@
     return jnp.concatenate(pieces, axis=1)
 
 
-def span_forward(layers, rows, warm, speed, energy, send, ratios, partials, reaches):
+def span_forward(
+    layers, rows, breadth, warm_far, speed_far, energy_far,
+    send, warm, ratios, partials, reaches, speed, energy, arrived,
+):
+    halves = breadth // LANES
+    lines = layers * rows
     opens = (lax.axis_index("gx") == 0).astype(jnp.float32)
-
-    def coefficient_at(i):
-        warmth = warm[pl.ds(i, layers, stride=rows), :]
-        return wide([jnp.exp(slope * warmth) for slope in SLOPES])
-
-    def source_at(i):
-        where = pl.ds(i, layers, stride=rows)
-        warmth = warm[where, :]
-        return wide([warmth + energy[where, :], speed[where, :] + lifting_push * warmth])
-
-    def keep(i, ratio, partial, reach):
-        where = pl.ds(pl.multiple_of((pl.program_id(0) * rows + i) * layers, layers), layers)
-        ratios[where, :] = ratio
-        partials[where, :] = partial
-        reaches[where, :] = reach
-
-    values = block_sweep(rows, coefficient_at, source_at, span_strength, opens, keep)
-    for number, value in enumerate(values):
-        for pair in range(PAIRS):
-            send[pl.ds(pair * layers * SENT + number, layers, stride=SENT), :] = value[
-                :, pair * LANES : (pair + 1) * LANES
-            ]
+    copies = [
+        [
+            pltpu.make_async_copy(
+                far.at[:, h * LANES : (h + 1) * LANES], held_at.at[h * lines : (h + 1) * lines, :], arrived.at[h, k]
+            )
+            for k, (far, held_at) in enumerate(((warm_far, warm), (energy_far, energy), (speed_far, speed)))
+        ]
+        for h in range(halves)
+    ]
+    for some in copies:
+        for copy in some:
+            copy.start()
+    for h in range(halves):
+        for copy in copies[h]:
+            copy.wait()
+
+        def coefficient_at(i):
+            warmth = warm[pl.ds(h * lines + i, layers, stride=rows), :]
+            return wide([jnp.exp(slope * warmth) for slope in SLOPES])
+
+        def source_at(i):
+            where = pl.ds(h * lines + i, layers, stride=rows)
+            warmth = warm[where, :]
+            return wide([warmth + energy[where, :], speed[where, :] + lifting_push * warmth])
+
+        def keep(i, ratio, partial, reach):
+            where = slice((h * rows + i) * layers, (h * rows + i + 1) * layers)
+            ratios[where, :] = ratio
+            partials[where, :] = partial
+            reaches[where, :] = reach
+
+        values = block_sweep(rows, coefficient_at, source_at, span_strength, opens, keep)
+        for number, value in enumerate(values):
+            for pair in range(PAIRS):
+                start = (h * PAIRS + pair) * layers * SENT + number
+                send[pl.ds(start, layers, stride=SENT), :] = value[:, pair * LANES : (pair + 1) * LANES]
 
 
 def span_reduced(blocks, received, fluxes):
@@ -214,10 +234,10 @@
     groups = lines // group
     length = breadth // CHUNKS
     for h in range(halves):
-        across = slice(h * LANES, (h + 1) * LANES)
         for g in range(groups):
+            start = h * lines + g * group
             turned_warm[g * breadth + h * LANES : g * breadth + (h + 1) * LANES, :] = warm[
-                g * group : (g + 1) * group, across
+                start : start + group, :
             ].T
     for h in range(halves):
         low, high = (
@@ -277,7 +297,9 @@
 ):
     received, refs = refs[:parts], refs[parts:]
     chunk_fluxes, ratios, partials, reaches, new_warmth, new_speed = refs[:6]
-    ordered, turned, solved, depth_ratios, depth_partials = refs[6:]
+    ordered, turned, solved, depth_ratios, depth_partials, *finished = refs[6:]
+    left = finished.pop()
+    copies = []
     halves = breadth // LANES
     lines = layers * rows
     group = min(LANES, lines)
@@ -316,11 +338,12 @@
             solved[number * group : (number + 1) * group, h * LANES : (h + 1) * LANES] = turned[
                 start : start + LANES, :
             ].T
-    for pair, out in enumerate((new_warmth, new_speed)):
+    for pair, (far, out) in enumerate(zip((new_warmth, new_speed), finished)):
         half = 0.5 * depth_strength
 
         def coefficient_at(z):
-            return jnp.exp(SLOPES[pair] * warm[z * rows : (z + 1) * rows, :])
+            starts = [h * lines + z * rows for h in range(halves)]
+            return jnp.exp(SLOPES[pair] * wide([warm[start : start + rows, :] for start in starts]))
 
         def source_at(z):
             return solved[pair * lines + z * rows : pair * lines + (z + 1) * rows, :]
@@ -346,6 +369,14 @@
             where = slice(z * rows, (z + 1) * rows)
             answer = depth_partials[where, :] + depth_ratios[where, :] * answer
             out[where, :] = answer
+            if z % PIECE == 0:
+                piece = pl.ds(z * rows, PIECE * rows)
+                copies.append(
+                    pltpu.make_async_copy(out.at[piece, :], far.at[piece, :], left.at[pair, z // PIECE])
+                )
+                copies[-1].start()
+    for copy in copies:
+        copy.wait()
 
 
 def shaped(*shape):
@@ -358,6 +389,10 @@
 
 def passed(*shape):
     return pltpu.VMEM(shape, jnp.float32)
+
+
+def distant(*values):
+    return [pltpu.with_memory_space_constraint(value, pltpu.HBM) for value in values]
 
 
 def near(*values):
@@ -376,19 +411,17 @@
     parts = lax.axis_size("gy")
     warm, speed, energy = (v.reshape(lines, breadth) for v in (prior_warmth, prior_speed, energy_input))
     kept = passed(halves * lines, PAIRS * LANES)
-    column_spec = pl.BlockSpec((lines, LANES), lambda h: (0, h))
-    kept_spec = pl.BlockSpec(memory_space=pltpu.VMEM)
-    send_rows = PAIRS * layers * SENT
-    send, ratios, partials, reaches = pl.pallas_call(
-        functools.partial(span_forward, layers, rows),
-        grid=(halves,),
-        in_specs=[column_spec] * 3,
-        out_specs=(pl.BlockSpec((send_rows, LANES), lambda h: (h, 0)), kept_spec, kept_spec, kept_spec),
-        out_shape=(shaped(blocks * SENT, LANES), kept, kept, kept),
+    column = (halves * lines, LANES)
+    far = pl.BlockSpec(memory_space=pltpu.HBM)
+    send, warm, ratios, partials, reaches = pl.pallas_call(
+        functools.partial(span_forward, layers, rows, breadth),
+        in_specs=[far] * 3,
+        out_shape=(passed(blocks * SENT, LANES), passed(*column), kept, kept, kept),
+        scratch_shapes=[held(*column), held(*column), pltpu.SemaphoreType.DMA((halves, 3))],
         name="span_forward",
         compiler_params=pltpu.CompilerParams(vmem_limit_bytes=ROOM),
         interpret=INTERPRET,
-    )(warm, speed, energy)
+    )(*distant(warm, speed, energy))
     received = lax.all_to_all(
         send.reshape(blocks, SENT, LANES), "gx", split_axis=0, concat_axis=0, tiled=True
     )
@@ -425,12 +458,16 @@
     finished = pl.pallas_call(
         functools.partial(cross_back_depth, layers, rows, breadth, parts),
         out_shape=(out, out),
+        out_specs=(far, far),
         scratch_shapes=[
             held(parts * SENT, PAIRS * lines),
             held(PAIRS * lines // group * breadth, group),
             held(PAIRS * lines, breadth),
             held(lines, breadth),
             held(lines, breadth),
+            held(lines, breadth),
+            held(lines, breadth),
+            pltpu.SemaphoreType.DMA((PAIRS, layers // PIECE)),
         ],
         name="cross_back_depth",
         compiler_params=pltpu.CompilerParams(vmem_limit_bytes=ROOM),

time: 55 us -> 52.9 us (0.962)
  local copies, waits for them, and re-layouts: 2.85 us -> 0 us
  Pallas kernels: 3.56 us -> 4.4 us
    unnamed x8 -> x0, local copies, waits for them, and re-layouts: 2.85 us -> none
    pallas_call x1, Pallas kernels: 0.78 us -> 1.6 us  [body(): pl.pallas_call(functools.partial(span_forward, layers, rows, breadth), in...]
where the time goes in v3:
time: 52.9 us; the launch traced here: 52.7 us
  blocking collectives  40.5 us (77%)
  Pallas kernels  4.4 us (8%)
  starting transfers between devices  3.85 us (7%)
  waiting for transfers between devices  3.23 us (6%)
  between operations  0.65 us (1%)
    all_to_all x1, blocking collectives, body(): lax.all_to_all(send.reshape(blocks, SENT, LANES), 'gx', split_axis=0, con...  25.9 us
    all_to_all x1, blocking collectives, body(): lax.all_to_all(flux.reshape(blocks, SIDES, LANES), 'gx', split_axis=0, co...  14.6 us
    ppermute x3, starting transfers between devices, body(): lax.ppermute(send, 'gy', [(i, (i + steps) % parts) for i in range(parts)])  3.85 us
    ppermute x3, waiting for transfers between devices, body(): lax.ppermute(send, 'gy', [(i, (i + steps) % parts) for i in range(parts)])  3.23 us
    pallas_call x1, Pallas kernels, body(): pl.pallas_call(functools.partial(span_forward, layers, rows, breadth), in...  1.6 us
    pallas_call x1, Pallas kernels, body(): pl.pallas_call(functools.partial(cross_back_depth, layers, rows, breadth,...  1.45 us
    pallas_call x1, Pallas kernels, body(): pl.pallas_call(functools.partial(span_back_cross_forward, layers, rows, b...  1.17 us
  transfers between devices with their start and end apart: 3, of which 2 were waited for; matrix products, arithmetic and copies ran while one was open for 0% of the time, Pallas kernels for 0%

profile of v3, /device:TPU:1, one launch (start us, length us, event | category | flops | bytes accessed | tf_op | source)
XLA Modules:
  0.0 52.7 jit_solution(5616893630243781900)
XLA Ops:
  0.6 1.6 %span_forward.1 = (f32[512,128]{1,0:T(8,128)S(1)}, f32[512,128]{1,0:T(8,128)S(1)}, f32[512,256]{1,0:T(8,128)S(1)}, f32[512,256]{1,0:T(8,128)S(1)}, f32[512,256]{1,0:T(8,128)S(1)}) custom-call(f32[256,256]{1,0:T(8,128)} %bitcast.13, f32[256,256]{1,0:T(8,128)} %bitcast.14, f32[256,256]{1,0:T(8,128)} %bitcast.15), custom_call_target="tpu_custom_call" | custom-call | tf_op jit(solution)/shard_map/span_forward/pallas_call | solution.py:416
  2.2 25.9 %all_to_all.10 = f32[64,8,128]{2,1,0:T(8,128)S(1)} all-to-all(f32[64,8,128]{2,1,0:T(8,128)S(1)} %bitcast.11), channel_id=1, replica_groups=mesh['gx'=64,'gy'=4] {'gx'}, dimensions={0} | all-to-all | bytes 524288 | tf_op jit(solution)/shard_map/all_to_all | solution.py:425
  28.2 0.2 span_reduced.1
  28.4 14.6 %all_to_all.11 = f32[64,2,128]{2,1,0:T(2,128)S(1)} all-to-all(f32[64,2,128]{2,1,0:T(2,128)S(1)} %bitcast.10), channel_id=1, replica_groups=mesh['gx'=64,'gy'=4] {'gx'}, dimensions={0} | all-to-all | bytes 131072 | tf_op jit(solution)/shard_map/all_to_all | solution.py:435
  43.0 1.2 %span_back_cross_forward.1 = (f32[8,512]{1,0:T(8,128)S(1)}, f32[24,512]{1,0:T(8,128)S(1)}, f32[256,512]{1,0:T(8,128)S(1)}, f32[256,512]{1,0:T(8,128)S(1)}, f32[256,512]{1,0:T(8,128)S(1)}) custom-call(f32[512,128]{1,0:T(8,128)S(1)} %get-tuple-element.14.warm, f32[128,128]{1,0:T(8,128)S(1)} %bitcast.12, f32[512,256]{1,0:T(8,128)S(1)} %get-tuple-element.16.ratios, ...), custom_call_target="tpu_custom_call" | custom-call | tf_op jit(solution)/shard_map/span_back_cross_forward/pallas_call | solution.py:439
  44.1 2.8 %collective-permute-start.2 = (f32[8,512]{1,0:T(8,128)S(1)}, f32[8,512]{1,0:T(8,128)S(1)}, u32[]{:S(2)}, u32[]{:S(2)}) collective-permute-start(f32[8,512]{1,0:T(8,128)S(1)} %get-tuple-element.19.refs_0_), channel_id=1, source_target_pairs={{0,3},{1,0},{2,1},{3,2},{4,7},{5,4},{6,5},{7,6},{8,11},{9,8},{10,9... | collective-permute-start | bytes 49160 | tf_op jit(solution)/shard_map/ppermute | solution.py:454
  47.0 0.3 collective-permute-start.1
  47.3 0.7 %collective-permute-start = (f32[8,512]{1,0:T(8,128)S(1)}, f32[8,512]{1,0:T(8,128)S(1)}, u32[]{:S(2)}, u32[]{:S(2)}) collective-permute-start(f32[8,512]{1,0:T(8,128)S(1)} %get-tuple-element.19.refs_0_), channel_id=1, source_target_pairs={{0,1},{1,2},{2,3},{3,0},{4,5},{5,6},{6,7},{7,4},{8,9},{9,10},{10,1... | collective-permute-start | bytes 49160 | tf_op jit(solution)/shard_map/ppermute | solution.py:454
  48.0 0.0 collective-permute-done.2.refs_3_
  48.0 3.1 %collective-permute-done.1.refs_2_ = f32[8,512]{1,0:T(8,128)S(1)} collective-permute-done((f32[8,512]{1,0:T(8,128)S(1)}, f32[8,512]{1,0:T(8,128)S(1)}, u32[]{:S(2)}, u32[]{:S(2)}) %collective-permute-start.1) | collective-permute-done | bytes 16416 | tf_op jit(solution)/shard_map/ppermute | solution.py:454
  51.1 0.2 collective-permute-done.refs_1_
  51.2 1.5 %cross_back_depth.1 = (f32[256,256]{1,0:T(8,128)}, f32[256,256]{1,0:T(8,128)}) custom-call(f32[512,128]{1,0:T(8,128)S(1)} %get-tuple-element.14.warm, f32[8,512]{1,0:T(8,128)S(1)} %get-tuple-element.19.refs_0_, f32[8,512]{1,0:T(8,128)S(1)} %collective-permute-done.refs_1_, f32[8,512]{1,0:T(8,128)S(1)} %collective-permute-done.1.refs_2_, ...), custom_call_target="tpu_custom_call" | custom-call | tf_op jit(solution)/shard_map/cross_back_depth/pallas_call | solution.py:458
Async XLA Ops:
  44.1 3.9 %collective-permute-start.2 = (f32[8,512]{1,0:T(8,128)S(1)}, f32[8,512]{1,0:T(8,128)S(1)}, u32[]{:S(2)}, u32[]{:S(2)}) collective-permute-start(f32[8,512]{1,0:T(8,128)S(1)} %get-tuple-element.19.refs_0_), channel_id=1, source_target_pairs={{0,3},{1,0},{2,1},{3,2},{4,7},{5,4},{6,5},{7,6},{8,11},{9,8},{10,9... | collective-permute-start | bytes 49160 | tf_op jit(solution)/shard_map/ppermute | solution.py:454
  47.0 4.1 %collective-permute-start.1 = (f32[8,512]{1,0:T(8,128)S(1)}, f32[8,512]{1,0:T(8,128)S(1)}, u32[]{:S(2)}, u32[]{:S(2)}) collective-permute-start(f32[8,512]{1,0:T(8,128)S(1)} %get-tuple-element.19.refs_0_), channel_id=1, source_target_pairs={{0,2},{1,3},{2,0},{3,1},{4,6},{5,7},{6,4},{7,5},{8,10},{9,11},{10,... | collective-permute-start | bytes 49160 | tf_op jit(solution)/shard_map/ppermute | solution.py:454
  47.3 3.9 %collective-permute-start = (f32[8,512]{1,0:T(8,128)S(1)}, f32[8,512]{1,0:T(8,128)S(1)}, u32[]{:S(2)}, u32[]{:S(2)}) collective-permute-start(f32[8,512]{1,0:T(8,128)S(1)} %get-tuple-element.19.refs_0_), channel_id=1, source_target_pairs={{0,1},{1,2},{2,3},{3,0},{4,5},{5,6},{6,7},{7,4},{8,9},{9,10},{10,1... | collective-permute-start | bytes 49160 | tf_op jit(solution)/shard_map/ppermute | solution.py:454

commit v4 on v3

--- a/solution.py
+++ b/solution.py
@@ -20,6 +20,7 @@
 CHUNKS = 8
 SENT = 8
 SIDES = 2
+SPAN_SENT = 6
 PIECE = 4
 ROOM = 24 * 2**20
 CROSS_SENT = 7
@@ -168,6 +169,18 @@
     return low, high
 
 
+def left_half(like):
+    return lax.broadcasted_iota(jnp.int32, like.shape, 1) < LANES // 2
+
+
+def cross_halves(one, other):
+    left = left_half(one)
+    return (
+        jnp.where(left, one, pltpu.roll(other, LANES // 2, 1)),
+        jnp.where(left, pltpu.roll(one, LANES // 2, 1), other),
+    )
+
+
 def wide(pieces):
     return jnp.concatenate(pieces, axis=1)
 
@@ -210,15 +223,22 @@
             partials[where, :] = partial
             reaches[where, :] = reach
 
-        values = block_sweep(rows, coefficient_at, source_at, span_strength, opens, keep)
-        for number, value in enumerate(values):
-            for pair in range(PAIRS):
-                start = (h * PAIRS + pair) * layers * SENT + number
-                send[pl.ds(start, layers, stride=SENT), :] = value[:, pair * LANES : (pair + 1) * LANES]
+        values = block_sweep(rows, coefficient_at, source_at, span_strength, opens, keep)[:5]
+        sides = [(value[:, :LANES], value[:, LANES:]) for value in values]
+        sides.append(tuple(warm[pl.ds(h * lines + i, layers, stride=rows), :] for i in (0, rows - 1)))
+        for number, (one, other) in enumerate(sides):
+            for part, value in enumerate(cross_halves(one, other)):
+                start = (h * PAIRS + part) * layers * SPAN_SENT + number
+                send[pl.ds(start, layers, stride=SPAN_SENT), :] = value
 
 
 def span_reduced(blocks, received, fluxes):
-    values = [received[pl.ds(number, blocks, stride=SENT), :] for number in range(CROSS_SENT)]
+    values = [received[pl.ds(number, blocks, stride=SPAN_SENT), :] for number in range(SPAN_SENT)]
+    edges = values.pop()
+    left = left_half(edges)
+    turned = pltpu.roll(edges, LANES // 2, 1)
+    slope = jnp.where(left, SLOPES[0], SLOPES[1])
+    values += [jnp.exp(slope * jnp.where(left, one, other)) for one, other in ((edges, turned), (turned, edges))]
     low, high = interface_flux(values, span_strength, blocks)
     fluxes[pl.ds(0, blocks, stride=SIDES), :] = low
     fluxes[pl.ds(1, blocks, stride=SIDES), :] = high
@@ -241,10 +261,10 @@
             ].T
     for h in range(halves):
         low, high = (
-            wide([
-                flux[pl.ds((h * PAIRS + pair) * layers * SIDES + side, layers, stride=SIDES), :]
-                for pair in range(PAIRS)
-            ])
+            wide(cross_halves(*(
+                flux[pl.ds((h * PAIRS + part) * layers * SIDES + side, layers, stride=SIDES), :]
+                for part in range(PAIRS)
+            )))
             for side in range(SIDES)
         )
 
@@ -306,9 +326,9 @@
     groups = lines // group
     length = breadth // CHUNKS
     own = lax.axis_index("gy")
-    for steps in range(parts):
+    for number, steps in enumerate(by_distance(parts)):
         slot = lax.rem(own + parts - steps, parts)
-        ordered[pl.ds(pl.multiple_of(slot * SENT, SENT), SENT), :] = received[steps][...]
+        ordered[pl.ds(pl.multiple_of(slot * SENT, SENT), SENT), :] = received[number][...]
     parts_values = [
         [ordered[d * SENT + number : d * SENT + number + 1, :] for number in range(CROSS_SENT)]
         for d in range(parts)
@@ -379,6 +399,10 @@
         copy.wait()
 
 
+def by_distance(parts):
+    return sorted(range(parts), key=lambda steps: min(steps, parts - steps))
+
+
 def shaped(*shape):
     return jax.ShapeDtypeStruct(shape, jnp.float32)
 
@@ -416,14 +440,14 @@
     send, warm, ratios, partials, reaches = pl.pallas_call(
         functools.partial(span_forward, layers, rows, breadth),
         in_specs=[far] * 3,
-        out_shape=(passed(blocks * SENT, LANES), passed(*column), kept, kept, kept),
+        out_shape=(passed(blocks * SPAN_SENT, LANES), passed(*column), kept, kept, kept),
         scratch_shapes=[held(*column), held(*column), pltpu.SemaphoreType.DMA((halves, 3))],
         name="span_forward",
         compiler_params=pltpu.CompilerParams(vmem_limit_bytes=ROOM),
         interpret=INTERPRET,
     )(*distant(warm, speed, energy))
     received = lax.all_to_all(
-        send.reshape(blocks, SENT, LANES), "gx", split_axis=0, concat_axis=0, tiled=True
+        send.reshape(-1, SIDES, LANES), "gx", split_axis=0, concat_axis=0, tiled=True
     )
     flux = pl.pallas_call(
         functools.partial(span_reduced, blocks),
@@ -431,7 +455,7 @@
         name="span_reduced",
         compiler_params=pltpu.CompilerParams(vmem_limit_bytes=ROOM),
         interpret=INTERPRET,
-    )(*near(received.reshape(blocks * SENT, LANES)))
+    )(*near(received.reshape(blocks * SPAN_SENT, LANES)))
     flux = lax.all_to_all(
         flux.reshape(blocks, SIDES, LANES), "gx", split_axis=0, concat_axis=0, tiled=True
     ).reshape(blocks * SIDES, LANES)
@@ -450,9 +474,9 @@
         compiler_params=pltpu.CompilerParams(vmem_limit_bytes=ROOM),
         interpret=INTERPRET,
     )(*near(warm, flux, ratios, partials, reaches))
-    received = [send] + [
-        lax.ppermute(send, "gy", [(i, (i + steps) % parts) for i in range(parts)])
-        for steps in range(1, parts)
+    received = [
+        lax.ppermute(send, "gy", [(i, (i + steps) % parts) for i in range(parts)]) if steps else send
+        for steps in by_distance(parts)
     ]
     out = shaped(lines, breadth)
     finished = pl.pallas_call(

time: 52.9 us -> 52.5 us (level)
  blocking collectives: 40.5 us -> 39.2 us
  starting transfers between devices: 3.85 us -> 4.47 us
  Pallas kernels: 4.4 us -> 4.93 us
    all_to_all x1, blocking collectives: 25.9 us -> 24.8 us  [body(): lax.all_to_all(send.reshape(-1, SIDES, LANES), 'gx', split_axis=0, concat...]
    ppermute x3, starting transfers between devices: 3.85 us -> 4.47 us  [body(): lax.ppermute(send, 'gy', [(i, (i + steps) % parts) for i in range(parts)])]
where the time goes in v4:
time: 52.5 us; the launch traced here: 52.3 us
  blocking collectives  39.2 us (75%)
  Pallas kernels  4.93 us (9%)
  starting transfers between devices  4.47 us (9%)
  waiting for transfers between devices  3.11 us (6%)
  between operations  0.65 us (1%)
    all_to_all x1, blocking collectives, body(): lax.all_to_all(send.reshape(-1, SIDES, LANES), 'gx', split_axis=0, concat...  24.8 us
    all_to_all x1, blocking collectives, body(): lax.all_to_all(flux.reshape(blocks, SIDES, LANES), 'gx', split_axis=0, co...  14.4 us
    ppermute x3, starting transfers between devices, body(): lax.ppermute(send, 'gy', [(i, (i + steps) % parts) for i in range(parts)])  4.47 us
    ppermute x3, waiting for transfers between devices, body(): lax.ppermute(send, 'gy', [(i, (i + steps) % parts) for i in range(parts)])  3.11 us
    pallas_call x1, Pallas kernels, body(): pl.pallas_call(functools.partial(span_forward, layers, rows, breadth), in...  1.88 us
    pallas_call x1, Pallas kernels, body(): pl.pallas_call(functools.partial(cross_back_depth, layers, rows, breadth,...  1.45 us
    pallas_call x1, Pallas kernels, body(): pl.pallas_call(functools.partial(span_back_cross_forward, layers, rows, b...  1.38 us
  transfers between devices with their start and end apart: 3, of which 2 were waited for; matrix products, arithmetic and copies ran while one was open for 0% of the time, Pallas kernels for 0%

profile of v4, /device:TPU:1, one launch (start us, length us, event | category | flops | bytes accessed | tf_op | source)
XLA Modules:
  0.0 52.3 jit_solution(15221891092064662018)
XLA Ops:
  0.6 1.9 %span_forward.1 = (f32[384,128]{1,0:T(8,128)S(1)}, f32[512,128]{1,0:T(8,128)S(1)}, f32[512,256]{1,0:T(8,128)S(1)}, f32[512,256]{1,0:T(8,128)S(1)}, f32[512,256]{1,0:T(8,128)S(1)}) custom-call(f32[256,256]{1,0:T(8,128)} %bitcast.13, f32[256,256]{1,0:T(8,128)} %bitcast.14, f32[256,256]{1,0:T(8,128)} %bitcast.15), custom_call_target="tpu_custom_call" | custom-call | tf_op jit(solution)/shard_map/span_forward/pallas_call | solution.py:440
  2.5 24.8 %all_to_all.10 = f32[192,2,128]{2,1,0:T(2,128)S(1)} all-to-all(f32[192,2,128]{2,1,0:T(2,128)S(1)} %bitcast.12), channel_id=1, replica_groups=mesh['gx'=64,'gy'=4] {'gx'}, dimensions={0} | all-to-all | bytes 393216 | tf_op jit(solution)/shard_map/all_to_all | solution.py:449
  27.3 0.2 span_reduced.1
  27.6 14.4 %all_to_all.11 = f32[64,2,128]{2,1,0:T(2,128)S(1)} all-to-all(f32[64,2,128]{2,1,0:T(2,128)S(1)} %bitcast.10), channel_id=1, replica_groups=mesh['gx'=64,'gy'=4] {'gx'}, dimensions={0} | all-to-all | bytes 131072 | tf_op jit(solution)/shard_map/all_to_all | solution.py:459
  41.9 1.4 %span_back_cross_forward.1 = (f32[8,512]{1,0:T(8,128)S(1)}, f32[24,512]{1,0:T(8,128)S(1)}, f32[256,512]{1,0:T(8,128)S(1)}, f32[256,512]{1,0:T(8,128)S(1)}, f32[256,512]{1,0:T(8,128)S(1)}) custom-call(f32[512,128]{1,0:T(8,128)S(1)} %get-tuple-element.14.warm, f32[128,128]{1,0:T(8,128)S(1)} %bitcast.11, f32[512,256]{1,0:T(8,128)S(1)} %get-tuple-element.16.ratios, ...), custom_call_target="tpu_custom_call" | custom-call | tf_op jit(solution)/shard_map/span_back_cross_forward/pallas_call | solution.py:463
  43.3 3.0 %collective-permute-start.2 = (f32[8,512]{1,0:T(8,128)S(1)}, f32[8,512]{1,0:T(8,128)S(1)}, u32[]{:S(2)}, u32[]{:S(2)}) collective-permute-start(f32[8,512]{1,0:T(8,128)S(1)} %get-tuple-element.19.refs_0_), channel_id=1, source_target_pairs={{0,2},{1,3},{2,0},{3,1},{4,6},{5,7},{6,4},{7,5},{8,10},{9,11},{10,... | collective-permute-start | bytes 49160 | tf_op jit(solution)/shard_map/ppermute | solution.py:478
  46.3 0.8 %collective-permute-start.1 = (f32[8,512]{1,0:T(8,128)S(1)}, f32[8,512]{1,0:T(8,128)S(1)}, u32[]{:S(2)}, u32[]{:S(2)}) collective-permute-start(f32[8,512]{1,0:T(8,128)S(1)} %get-tuple-element.19.refs_0_), channel_id=1, source_target_pairs={{0,3},{1,0},{2,1},{3,2},{4,7},{5,4},{6,5},{7,6},{8,11},{9,8},{10,9... | collective-permute-start | bytes 49160 | tf_op jit(solution)/shard_map/ppermute | solution.py:478
  47.1 0.7 %collective-permute-start = (f32[8,512]{1,0:T(8,128)S(1)}, f32[8,512]{1,0:T(8,128)S(1)}, u32[]{:S(2)}, u32[]{:S(2)}) collective-permute-start(f32[8,512]{1,0:T(8,128)S(1)} %get-tuple-element.19.refs_0_), channel_id=1, source_target_pairs={{0,1},{1,2},{2,3},{3,0},{4,5},{5,6},{6,7},{7,4},{8,9},{9,10},{10,1... | collective-permute-start | bytes 49160 | tf_op jit(solution)/shard_map/ppermute | solution.py:478
  47.8 0.0 collective-permute-done.2.refs_3_
  47.8 1.1 %collective-permute-done.1.refs_2_ = f32[8,512]{1,0:T(8,128)S(1)} collective-permute-done((f32[8,512]{1,0:T(8,128)S(1)}, f32[8,512]{1,0:T(8,128)S(1)}, u32[]{:S(2)}, u32[]{:S(2)}) %collective-permute-start.1) | collective-permute-done | bytes 16416 | tf_op jit(solution)/shard_map/ppermute | solution.py:478
  48.9 2.0 %collective-permute-done.refs_1_ = f32[8,512]{1,0:T(8,128)S(1)} collective-permute-done((f32[8,512]{1,0:T(8,128)S(1)}, f32[8,512]{1,0:T(8,128)S(1)}, u32[]{:S(2)}, u32[]{:S(2)}) %collective-permute-start) | collective-permute-done | bytes 16416 | tf_op jit(solution)/shard_map/ppermute | solution.py:478
  50.9 1.5 %cross_back_depth.1 = (f32[256,256]{1,0:T(8,128)}, f32[256,256]{1,0:T(8,128)}) custom-call(f32[512,128]{1,0:T(8,128)S(1)} %get-tuple-element.14.warm, f32[8,512]{1,0:T(8,128)S(1)} %get-tuple-element.19.refs_0_, f32[8,512]{1,0:T(8,128)S(1)} %collective-permute-done.refs_1_, f32[8,512]{1,0:T(8,128)S(1)} %collective-permute-done.1.refs_2_, ...), custom_call_target="tpu_custom_call" | custom-call | tf_op jit(solution)/shard_map/cross_back_depth/pallas_call | solution.py:482
Async XLA Ops:
  43.3 4.5 %collective-permute-start.2 = (f32[8,512]{1,0:T(8,128)S(1)}, f32[8,512]{1,0:T(8,128)S(1)}, u32[]{:S(2)}, u32[]{:S(2)}) collective-permute-start(f32[8,512]{1,0:T(8,128)S(1)} %get-tuple-element.19.refs_0_), channel_id=1, source_target_pairs={{0,2},{1,3},{2,0},{3,1},{4,6},{5,7},{6,4},{7,5},{8,10},{9,11},{10,... | collective-permute-start | bytes 49160 | tf_op jit(solution)/shard_map/ppermute | solution.py:478
  46.3 2.6 %collective-permute-start.1 = (f32[8,512]{1,0:T(8,128)S(1)}, f32[8,512]{1,0:T(8,128)S(1)}, u32[]{:S(2)}, u32[]{:S(2)}) collective-permute-start(f32[8,512]{1,0:T(8,128)S(1)} %get-tuple-element.19.refs_0_), channel_id=1, source_target_pairs={{0,3},{1,0},{2,1},{3,2},{4,7},{5,4},{6,5},{7,6},{8,11},{9,8},{10,9... | collective-permute-start | bytes 49160 | tf_op jit(solution)/shard_map/ppermute | solution.py:478
  47.1 3.8 %collective-permute-start = (f32[8,512]{1,0:T(8,128)S(1)}, f32[8,512]{1,0:T(8,128)S(1)}, u32[]{:S(2)}, u32[]{:S(2)}) collective-permute-start(f32[8,512]{1,0:T(8,128)S(1)} %get-tuple-element.19.refs_0_), channel_id=1, source_target_pairs={{0,1},{1,2},{2,3},{3,0},{4,5},{5,6},{6,7},{7,4},{8,9},{9,10},{10,1... | collective-permute-start | bytes 49160 | tf_op jit(solution)/shard_map/ppermute | solution.py:478

commit v5 on v4

--- a/solution.py
+++ b/solution.py
@@ -20,6 +20,7 @@
 CHUNKS = 8
 SENT = 8
 SIDES = 2
+TRADED = 3
 SPAN_SENT = 6
 PIECE = 4
 ROOM = 24 * 2**20
@@ -312,10 +313,39 @@
         send[number : number + 1, :] = value
 
 
+def cross_pair(mine, partner, merged):
+    even = lax.rem(lax.axis_index("gy"), 2) == 0
+    lower = jnp.where(even, mine[...], partner[...])
+    upper = jnp.where(even, partner[...], mine[...])
+    low_first, low_last, low_reach, low_cross, low_end, low_q, low_q_last = (
+        lower[number : number + 1, :] for number in range(CROSS_SENT)
+    )
+    high_first, high_last, high_reach, high_cross, high_end, high_q, high_q_last = (
+        upper[number : number + 1, :] for number in range(CROSS_SENT)
+    )
+    face = 0.5 * cross_strength * (low_q_last + high_q)
+    scale = face / (1.0 + face * (low_end + high_reach))
+    fixed = scale * (low_last - high_first)
+    by_low = scale * low_cross
+    by_high = scale * high_cross
+    values = (
+        low_first - low_cross * fixed,
+        high_last + high_cross * fixed,
+        low_reach - low_cross * by_low,
+        high_cross * by_low,
+        high_end - high_cross * by_high,
+        low_q,
+        high_q_last,
+        high_q_last,
+    )
+    for number, value in enumerate(values):
+        merged[number : number + 1, :] = value
+
+
 def cross_back_depth(
-    layers, rows, breadth, parts, warm, *refs
+    layers, rows, breadth, warm, *refs
 ):
-    received, refs = refs[:parts], refs[parts:]
+    received, refs = refs[:TRADED], refs[TRADED:]
     chunk_fluxes, ratios, partials, reaches, new_warmth, new_speed = refs[:6]
     ordered, turned, solved, depth_ratios, depth_partials, *finished = refs[6:]
     left = finished.pop()
@@ -326,14 +356,16 @@
     groups = lines // group
     length = breadth // CHUNKS
     own = lax.axis_index("gy")
-    for number, steps in enumerate(by_distance(parts)):
-        slot = lax.rem(own + parts - steps, parts)
-        ordered[pl.ds(pl.multiple_of(slot * SENT, SENT), SENT), :] = received[number][...]
+    in_upper = own // 2
+    place = in_upper + lax.rem(own, 2)
+    slots = (place, in_upper + 1 - lax.rem(own, 2), 2 - 2 * in_upper)
+    for slot, block in zip(slots, received):
+        ordered[pl.ds(pl.multiple_of(slot * SENT, SENT), SENT), :] = block[...]
     parts_values = [
         [ordered[d * SENT + number : d * SENT + number + 1, :] for number in range(CROSS_SENT)]
-        for d in range(parts)
+        for d in range(TRADED)
     ]
-    end_low, end_high = own_flux(parts_values, cross_strength, own)
+    end_low, end_high = own_flux(parts_values, cross_strength, place)
     fixed, by_low, by_high = (
         chunk_fluxes[number * CHUNKS : (number + 1) * CHUNKS, :] for number in range(3)
     )
@@ -399,10 +431,6 @@
         copy.wait()
 
 
-def by_distance(parts):
-    return sorted(range(parts), key=lambda steps: min(steps, parts - steps))
-
-
 def shaped(*shape):
     return jax.ShapeDtypeStruct(shape, jnp.float32)
 
@@ -474,17 +502,23 @@
         compiler_params=pltpu.CompilerParams(vmem_limit_bytes=ROOM),
         interpret=INTERPRET,
     )(*near(warm, flux, ratios, partials, reaches))
-    received = [
-        lax.ppermute(send, "gy", [(i, (i + steps) % parts) for i in range(parts)]) if steps else send
-        for steps in by_distance(parts)
-    ]
+    partner = lax.ppermute(send, "gy", [(i, i ^ 1) for i in range(parts)])
+    pair_block = pl.pallas_call(
+        cross_pair,
+        out_shape=passed(SENT, PAIRS * lines),
+        name="cross_pair",
+        compiler_params=pltpu.CompilerParams(vmem_limit_bytes=ROOM),
+        interpret=INTERPRET,
+    )(*near(send, partner))
+    other_pair = lax.ppermute(pair_block, "gy", [(i, i ^ 3) for i in range(parts)])
+    received = [send, partner, other_pair]
     out = shaped(lines, breadth)
     finished = pl.pallas_call(
-        functools.partial(cross_back_depth, layers, rows, breadth, parts),
+        functools.partial(cross_back_depth, layers, rows, breadth),
         out_shape=(out, out),
         out_specs=(far, far),
         scratch_shapes=[
-            held(parts * SENT, PAIRS * lines),
+            held(TRADED * SENT, PAIRS * lines),
             held(PAIRS * lines // group * breadth, group),
             held(PAIRS * lines, breadth),
             held(lines, breadth),

time: 52.5 us -> 52.7 us (level)
  the two profiles are of different devices: /device:TPU:1 before, /device:TPU:24 now
where the time goes in v5:
time: 52.7 us; the launch traced here: 52.5 us
  blocking collectives  38.1 us (72%)
  waiting for transfers between devices  7.72 us (15%)
  Pallas kernels  4.96 us (9%)
  starting transfers between devices  1.14 us (2%)
  between operations  0.66 us (1%)
    all_to_all x1, blocking collectives, body(): lax.all_to_all(send.reshape(-1, SIDES, LANES), 'gx', split_axis=0, concat...  23.7 us
    all_to_all x1, blocking collectives, body(): lax.all_to_all(flux.reshape(blocks, SIDES, LANES), 'gx', split_axis=0, co...  14.4 us
    ppermute x1, waiting for transfers between devices, body(): lax.ppermute(pair_block, 'gy', [(i, i ^ 3) for i in range(parts)])  4.73 us
    ppermute x1, waiting for transfers between devices, body(): partner = lax.ppermute(send, 'gy', [(i, i ^ 1) for i in range(parts)])  3 us
    pallas_call x1, Pallas kernels, body(): pl.pallas_call(functools.partial(span_forward, layers, rows, breadth), in...  1.88 us
    pallas_call x1, Pallas kernels, body(): pl.pallas_call(functools.partial(cross_back_depth, layers, rows, breadth)...  1.44 us
    pallas_call x1, Pallas kernels, body(): pl.pallas_call(functools.partial(span_back_cross_forward, layers, rows, b...  1.38 us
  transfers between devices with their start and end apart: 2, of which 2 were waited for; matrix products, arithmetic and copies ran while one was open for 0% of the time, Pallas kernels for 0%

profile of v5, /device:TPU:24, one launch (start us, length us, event | category | flops | bytes accessed | tf_op | source)
XLA Modules:
  0.0 52.5 jit_solution(13517940673099983051)
XLA Ops:
  0.6 1.9 %span_forward.1 = (f32[384,128]{1,0:T(8,128)S(1)}, f32[512,128]{1,0:T(8,128)S(1)}, f32[512,256]{1,0:T(8,128)S(1)}, f32[512,256]{1,0:T(8,128)S(1)}, f32[512,256]{1,0:T(8,128)S(1)}) custom-call(f32[256,256]{1,0:T(8,128)} %bitcast.13, f32[256,256]{1,0:T(8,128)} %bitcast.14, f32[256,256]{1,0:T(8,128)} %bitcast.15), custom_call_target="tpu_custom_call" | custom-call | tf_op jit(solution)/shard_map/span_forward/pallas_call | solution.py:468
  2.5 23.7 %all_to_all.10 = f32[192,2,128]{2,1,0:T(2,128)S(1)} all-to-all(f32[192,2,128]{2,1,0:T(2,128)S(1)} %bitcast.12), channel_id=1, replica_groups=mesh['gx'=64,'gy'=4] {'gx'}, dimensions={0} | all-to-all | bytes 393216 | tf_op jit(solution)/shard_map/all_to_all | solution.py:477
  26.2 0.2 span_reduced.1
  26.4 14.4 %all_to_all.11 = f32[64,2,128]{2,1,0:T(2,128)S(1)} all-to-all(f32[64,2,128]{2,1,0:T(2,128)S(1)} %bitcast.10), channel_id=1, replica_groups=mesh['gx'=64,'gy'=4] {'gx'}, dimensions={0} | all-to-all | bytes 131072 | tf_op jit(solution)/shard_map/all_to_all | solution.py:487
  40.8 1.4 %span_back_cross_forward.1 = (f32[8,512]{1,0:T(8,128)S(1)}, f32[24,512]{1,0:T(8,128)S(1)}, f32[256,512]{1,0:T(8,128)S(1)}, f32[256,512]{1,0:T(8,128)S(1)}, f32[256,512]{1,0:T(8,128)S(1)}) custom-call(f32[512,128]{1,0:T(8,128)S(1)} %get-tuple-element.14.warm, f32[128,128]{1,0:T(8,128)S(1)} %bitcast.11, f32[512,256]{1,0:T(8,128)S(1)} %get-tuple-element.16.ratios, ...), custom_call_target="tpu_custom_call" | custom-call | tf_op jit(solution)/shard_map/span_back_cross_forward/pallas_call | solution.py:491
  42.2 0.8 %collective-permute-start = (f32[8,512]{1,0:T(8,128)S(1)}, f32[8,512]{1,0:T(8,128)S(1)}, u32[]{:S(2)}, u32[]{:S(2)}) collective-permute-start(f32[8,512]{1,0:T(8,128)S(1)} %get-tuple-element.19.mine.refs_0_), channel_id=1, source_target_pairs={{0,1},{1,0},{2,3},{3,2},{4,5},{5,4},{6,7},{7,6},{8,9},{9,8},{10,11... | collective-permute-start | bytes 49160 | tf_op jit(solution)/shard_map/ppermute | solution.py:505
  43.0 3.0 %collective-permute-done.partner.refs_1_ = f32[8,512]{1,0:T(8,128)S(1)} collective-permute-done((f32[8,512]{1,0:T(8,128)S(1)}, f32[8,512]{1,0:T(8,128)S(1)}, u32[]{:S(2)}, u32[]{:S(2)}) %collective-permute-start) | collective-permute-done | bytes 16416 | tf_op jit(solution)/shard_map/ppermute | solution.py:505
  46.0 0.3 collective-permute-start.1
  46.4 4.7 %collective-permute-done.1.refs_2_ = f32[8,512]{1,0:T(8,128)S(1)} collective-permute-done((f32[8,512]{1,0:T(8,128)S(1)}, f32[8,512]{1,0:T(8,128)S(1)}, u32[]{:S(2)}, u32[]{:S(2)}) %collective-permute-start.1) | collective-permute-done | bytes 16416 | tf_op jit(solution)/shard_map/ppermute | solution.py:513
  51.1 1.4 %cross_back_depth.1 = (f32[256,256]{1,0:T(8,128)}, f32[256,256]{1,0:T(8,128)}) custom-call(f32[512,128]{1,0:T(8,128)S(1)} %get-tuple-element.14.warm, f32[8,512]{1,0:T(8,128)S(1)} %get-tuple-element.19.mine.refs_0_, f32[8,512]{1,0:T(8,128)S(1)} %collective-permute-done.partner.refs_1_, f32[8,512]{1,0:T(8,128)S(1)} %collective-permute-done.1.refs_2_, ...), custom_call_target="tpu_custom_call" | custom-call | tf_op jit(solution)/shard_map/cross_back_depth/pallas_call | solution.py:516
  (1 shorter events, 0.0 us)
Async XLA Ops:
  42.2 3.8 %collective-permute-start = (f32[8,512]{1,0:T(8,128)S(1)}, f32[8,512]{1,0:T(8,128)S(1)}, u32[]{:S(2)}, u32[]{:S(2)}) collective-permute-start(f32[8,512]{1,0:T(8,128)S(1)} %get-tuple-element.19.mine.refs_0_), channel_id=1, source_target_pairs={{0,1},{1,0},{2,3},{3,2},{4,5},{5,4},{6,7},{7,6},{8,9},{9,8},{10,11... | collective-permute-start | bytes 49160 | tf_op jit(solution)/shard_map/ppermute | solution.py:505
  46.0 5.0 %collective-permute-start.1 = (f32[8,512]{1,0:T(8,128)S(1)}, f32[8,512]{1,0:T(8,128)S(1)}, u32[]{:S(2)}, u32[]{:S(2)}) collective-permute-start(f32[8,512]{1,0:T(8,128)S(1)} %cross_pair.1), channel_id=1, source_target_pairs={{0,3},{1,2},{2,1},{3,0},{4,7},{5,6},{6,5},{7,4},{8,11},{9,10},{10,... | collective-permute-start | bytes 49160 | tf_op jit(solution)/shard_map/ppermute | solution.py:513

commit v6 on v4

--- a/solution.py
+++ b/solution.py
@@ -312,12 +312,44 @@
         send[number : number + 1, :] = value
 
 
+def depth_factors(layers, rows, breadth, warm, chunk_fluxes, inverses, ratios, carries):
+    halves = breadth // LANES
+    lines = layers * rows
+    half = 0.5 * depth_strength
+    for pair in range(PAIRS):
+
+        def coefficient_at(z):
+            starts = [h * lines + z * rows for h in range(halves)]
+            return jnp.exp(SLOPES[pair] * wide([warm[start : start + rows, :] for start in starts]))
+
+        q_now = coefficient_at(0)
+        delta = 1.0 + half * q_now
+        face_before = None
+        for z in range(layers):
+            where = slice(pair * lines + z * rows, pair * lines + (z + 1) * rows)
+            if z < layers - 1:
+                q_next = coefficient_at(z + 1)
+                face = half * (q_now + q_next)
+            else:
+                q_next, face = q_now, half * q_now
+            inverse = 1.0 / (delta + face)
+            inverses[where, :] = inverse
+            if face_before is not None:
+                carries[where, :] = face_before * inverse
+            ratio = face * inverse
+            if z < layers - 1:
+                ratios[where, :] = ratio
+                delta = 1.0 + delta * ratio
+            q_now, face_before = q_next, face
+
+
 def cross_back_depth(
-    layers, rows, breadth, parts, warm, *refs
+    layers, rows, breadth, parts, *refs
 ):
     received, refs = refs[:parts], refs[parts:]
-    chunk_fluxes, ratios, partials, reaches, new_warmth, new_speed = refs[:6]
-    ordered, turned, solved, depth_ratios, depth_partials, *finished = refs[6:]
+    chunk_fluxes, ratios, partials, reaches = refs[:4]
+    depth_inverses, depth_ratios, depth_carries, new_warmth, new_speed = refs[4:9]
+    ordered, turned, solved, depth_partials, *finished = refs[9:]
     left = finished.pop()
     copies = []
     halves = breadth // LANES
@@ -326,7 +358,7 @@
     groups = lines // group
     length = breadth // CHUNKS
     own = lax.axis_index("gy")
-    for number, steps in enumerate(by_distance(parts)):
+    for number, steps in enumerate(range(parts)):
         slot = lax.rem(own + parts - steps, parts)
         ordered[pl.ds(pl.multiple_of(slot * SENT, SENT), SENT), :] = received[number][...]
     parts_values = [
@@ -359,35 +391,20 @@
                 start : start + LANES, :
             ].T
     for pair, (far, out) in enumerate(zip((new_warmth, new_speed), finished)):
-        half = 0.5 * depth_strength
-
-        def coefficient_at(z):
-            starts = [h * lines + z * rows for h in range(halves)]
-            return jnp.exp(SLOPES[pair] * wide([warm[start : start + rows, :] for start in starts]))
-
-        def source_at(z):
-            return solved[pair * lines + z * rows : pair * lines + (z + 1) * rows, :]
-
-        q_now = coefficient_at(0)
-        numerator = source_at(0)
-        delta = 1.0 + half * q_now
-        for z in range(layers - 1):
-            where = slice(z * rows, (z + 1) * rows)
-            q_next = coefficient_at(z + 1)
-            face = half * (q_now + q_next)
-            inverse = 1.0 / (delta + face)
-            ratio = face * inverse
-            partial = numerator * inverse
-            depth_ratios[where, :] = ratio
-            depth_partials[where, :] = partial
-            delta = 1.0 + delta * ratio
-            numerator = source_at(z + 1) + face * partial
-            q_now = q_next
-        answer = numerator / (delta + half * q_now)
+        base = pair * lines
+        partial = None
+        for z in range(layers):
+            where = slice(base + z * rows, base + (z + 1) * rows)
+            fixed = solved[where, :] * depth_inverses[where, :]
+            partial = fixed if partial is None else fixed + depth_carries[where, :] * partial
+            if z < layers - 1:
+                depth_partials[z * rows : (z + 1) * rows, :] = partial
+        answer = partial
         out[(layers - 1) * rows : layers * rows, :] = answer
         for z in reversed(range(layers - 1)):
             where = slice(z * rows, (z + 1) * rows)
-            answer = depth_partials[where, :] + depth_ratios[where, :] * answer
+            ratio = depth_ratios[base + z * rows : base + (z + 1) * rows, :]
+            answer = depth_partials[where, :] + ratio * answer
             out[where, :] = answer
             if z % PIECE == 0:
                 piece = pl.ds(z * rows, PIECE * rows)
@@ -397,10 +414,6 @@
                 copies[-1].start()
     for copy in copies:
         copy.wait()
-
-
-def by_distance(parts):
-    return sorted(range(parts), key=lambda steps: min(steps, parts - steps))
 
 
 def shaped(*shape):
@@ -476,8 +489,15 @@
     )(*near(warm, flux, ratios, partials, reaches))
     received = [
         lax.ppermute(send, "gy", [(i, (i + steps) % parts) for i in range(parts)]) if steps else send
-        for steps in by_distance(parts)
+        for steps in range(parts)
     ]
+    factors = pl.pallas_call(
+        functools.partial(depth_factors, layers, rows, breadth),
+        out_shape=(passed(PAIRS * lines, breadth),) * 3,
+        name="depth_factors",
+        compiler_params=pltpu.CompilerParams(vmem_limit_bytes=ROOM),
+        interpret=INTERPRET,
+    )(*near(warm, chunk_fluxes))
     out = shaped(lines, breadth)
     finished = pl.pallas_call(
         functools.partial(cross_back_depth, layers, rows, breadth, parts),
@@ -490,13 +510,12 @@
             held(lines, breadth),
             held(lines, breadth),
             held(lines, breadth),
-            held(lines, breadth),
             pltpu.SemaphoreType.DMA((PAIRS, layers // PIECE)),
         ],
         name="cross_back_depth",
         compiler_params=pltpu.CompilerParams(vmem_limit_bytes=ROOM),
         interpret=INTERPRET,
-    )(*near(warm, *received, chunk_fluxes, *cross_kept))
+    )(*near(*received, chunk_fluxes, *cross_kept, *factors))
     return tuple(v.reshape(layers, rows, breadth) for v in finished)
 
 

time: 52.5 us -> 51.9 us (0.989)
  starting transfers between devices: 4.47 us -> 3.85 us
    ppermute x3, starting transfers between devices: 4.47 us -> 3.85 us  [body(): lax.ppermute(send, 'gy', [(i, (i + steps) % parts) for i in range(parts)])]
where the time goes in v6:
time: 51.9 us; the launch traced here: 51.8 us
  blocking collectives  39.2 us (76%)
  Pallas kernels  5.08 us (10%)
  starting transfers between devices  3.85 us (7%)
  waiting for transfers between devices  3 us (6%)
  between operations  0.66 us (1%)
    all_to_all x1, blocking collectives, body(): lax.all_to_all(send.reshape(-1, SIDES, LANES), 'gx', split_axis=0, concat...  24.8 us
    all_to_all x1, blocking collectives, body(): lax.all_to_all(flux.reshape(blocks, SIDES, LANES), 'gx', split_axis=0, co...  14.4 us
    ppermute x3, starting transfers between devices, body(): lax.ppermute(send, 'gy', [(i, (i + steps) % parts) for i in range(parts)])  3.85 us
    ppermute x3, waiting for transfers between devices, body(): lax.ppermute(send, 'gy', [(i, (i + steps) % parts) for i in range(parts)])  3 us
    pallas_call x1, Pallas kernels, body(): pl.pallas_call(functools.partial(span_forward, layers, rows, breadth), in...  1.88 us
    pallas_call x1, Pallas kernels, body(): pl.pallas_call(functools.partial(cross_back_depth, layers, rows, breadth,...  1.39 us
    pallas_call x1, Pallas kernels, body(): pl.pallas_call(functools.partial(span_back_cross_forward, layers, rows, b...  1.38 us
  transfers between devices with their start and end apart: 3, of which 2 were waited for; matrix products, arithmetic and copies ran while one was open for 0% of the time, Pallas kernels for 0%

profile of v6, /device:TPU:1, one launch (start us, length us, event | category | flops | bytes accessed | tf_op | source)
XLA Modules:
  0.0 51.8 jit_solution(11322644450312792204)
XLA Ops:
  0.6 1.9 %span_forward.1 = (f32[384,128]{1,0:T(8,128)S(1)}, f32[512,128]{1,0:T(8,128)S(1)}, f32[512,256]{1,0:T(8,128)S(1)}, f32[512,256]{1,0:T(8,128)S(1)}, f32[512,256]{1,0:T(8,128)S(1)}) custom-call(f32[256,256]{1,0:T(8,128)} %bitcast.13, f32[256,256]{1,0:T(8,128)} %bitcast.14, f32[256,256]{1,0:T(8,128)} %bitcast.15), custom_call_target="tpu_custom_call" | custom-call | tf_op jit(solution)/shard_map/span_forward/pallas_call | solution.py:453
  2.5 24.8 %all_to_all.10 = f32[192,2,128]{2,1,0:T(2,128)S(1)} all-to-all(f32[192,2,128]{2,1,0:T(2,128)S(1)} %bitcast.12), channel_id=1, replica_groups=mesh['gx'=64,'gy'=4] {'gx'}, dimensions={0} | all-to-all | bytes 393216 | tf_op jit(solution)/shard_map/all_to_all | solution.py:462
  27.3 0.2 span_reduced.1
  27.6 14.4 %all_to_all.11 = f32[64,2,128]{2,1,0:T(2,128)S(1)} all-to-all(f32[64,2,128]{2,1,0:T(2,128)S(1)} %bitcast.10), channel_id=1, replica_groups=mesh['gx'=64,'gy'=4] {'gx'}, dimensions={0} | all-to-all | bytes 131072 | tf_op jit(solution)/shard_map/all_to_all | solution.py:472
  41.9 1.4 %span_back_cross_forward.1 = (f32[8,512]{1,0:T(8,128)S(1)}, f32[24,512]{1,0:T(8,128)S(1)}, f32[256,512]{1,0:T(8,128)S(1)}, f32[256,512]{1,0:T(8,128)S(1)}, f32[256,512]{1,0:T(8,128)S(1)}) custom-call(f32[512,128]{1,0:T(8,128)S(1)} %get-tuple-element.17.warm, f32[128,128]{1,0:T(8,128)S(1)} %bitcast.11, f32[512,256]{1,0:T(8,128)S(1)} %get-tuple-element.19.ratios, ...), custom_call_target="tpu_custom_call" | custom-call | tf_op jit(solution)/shard_map/span_back_cross_forward/pallas_call | solution.py:476
  43.3 2.8 %collective-permute-start.2 = (f32[8,512]{1,0:T(8,128)S(1)}, f32[8,512]{1,0:T(8,128)S(1)}, u32[]{:S(2)}, u32[]{:S(2)}) collective-permute-start(f32[8,512]{1,0:T(8,128)S(1)} %get-tuple-element.22.refs_0_), channel_id=1, source_target_pairs={{0,3},{1,0},{2,1},{3,2},{4,7},{5,4},{6,5},{7,6},{8,11},{9,8},{10,9... | collective-permute-start | bytes 49160 | tf_op jit(solution)/shard_map/ppermute | solution.py:491
  46.1 0.3 collective-permute-start.1
  46.5 0.7 %collective-permute-start = (f32[8,512]{1,0:T(8,128)S(1)}, f32[8,512]{1,0:T(8,128)S(1)}, u32[]{:S(2)}, u32[]{:S(2)}) collective-permute-start(f32[8,512]{1,0:T(8,128)S(1)} %get-tuple-element.22.refs_0_), channel_id=1, source_target_pairs={{0,1},{1,2},{2,3},{3,0},{4,5},{5,6},{6,7},{7,4},{8,9},{9,10},{10,1... | collective-permute-start | bytes 49160 | tf_op jit(solution)/shard_map/ppermute | solution.py:491
  47.1 0.2 depth_factors.1
  47.4 0.0 collective-permute-done.2.refs_3_
  47.4 2.8 %collective-permute-done.1.refs_2_ = f32[8,512]{1,0:T(8,128)S(1)} collective-permute-done((f32[8,512]{1,0:T(8,128)S(1)}, f32[8,512]{1,0:T(8,128)S(1)}, u32[]{:S(2)}, u32[]{:S(2)}) %collective-permute-start.1) | collective-permute-done | bytes 16416 | tf_op jit(solution)/shard_map/ppermute | solution.py:491
  50.2 0.2 collective-permute-done.refs_1_
  50.4 1.4 %cross_back_depth.1 = (f32[256,256]{1,0:T(8,128)}, f32[256,256]{1,0:T(8,128)}) custom-call(f32[8,512]{1,0:T(8,128)S(1)} %get-tuple-element.22.refs_0_, f32[8,512]{1,0:T(8,128)S(1)} %collective-permute-done.refs_1_, f32[8,512]{1,0:T(8,128)S(1)} %collective-permute-done.1.refs_2_, f32[8,512]{1,0:T(8,128)S(1)} %collective-permute-done.2.refs_3_, ...), custom_call_target="tpu_custom_call" | custom-call | tf_op jit(solution)/shard_map/cross_back_depth/pallas_call | solution.py:502
Async XLA Ops:
  43.3 4.1 %collective-permute-start.2 = (f32[8,512]{1,0:T(8,128)S(1)}, f32[8,512]{1,0:T(8,128)S(1)}, u32[]{:S(2)}, u32[]{:S(2)}) collective-permute-start(f32[8,512]{1,0:T(8,128)S(1)} %get-tuple-element.22.refs_0_), channel_id=1, source_target_pairs={{0,3},{1,0},{2,1},{3,2},{4,7},{5,4},{6,5},{7,6},{8,11},{9,8},{10,9... | collective-permute-start | bytes 49160 | tf_op jit(solution)/shard_map/ppermute | solution.py:491
  46.1 4.1 %collective-permute-start.1 = (f32[8,512]{1,0:T(8,128)S(1)}, f32[8,512]{1,0:T(8,128)S(1)}, u32[]{:S(2)}, u32[]{:S(2)}) collective-permute-start(f32[8,512]{1,0:T(8,128)S(1)} %get-tuple-element.22.refs_0_), channel_id=1, source_target_pairs={{0,2},{1,3},{2,0},{3,1},{4,6},{5,7},{6,4},{7,5},{8,10},{9,11},{10,... | collective-permute-start | bytes 49160 | tf_op jit(solution)/shard_map/ppermute | solution.py:491
  46.5 3.9 %collective-permute-start = (f32[8,512]{1,0:T(8,128)S(1)}, f32[8,512]{1,0:T(8,128)S(1)}, u32[]{:S(2)}, u32[]{:S(2)}) collective-permute-start(f32[8,512]{1,0:T(8,128)S(1)} %get-tuple-element.22.refs_0_), channel_id=1, source_target_pairs={{0,1},{1,2},{2,3},{3,0},{4,5},{5,6},{6,7},{7,4},{8,9},{9,10},{10,1... | collective-permute-start | bytes 49160 | tf_op jit(solution)/shard_map/ppermute | solution.py:491
